TPU v7x, 32 devices: a whole 2x2x4 slice. The times are simulated.
32 devices in a mesh: wide: 8 (over z, y), narrow: 4 (over x, core).
Axes of the slice: x: 2, y: 2, z: 4, core: 2. Of those that a mesh axis runs over, the one named last changes fastest.
Arguments:
- activations: bfloat16 [256, 28672], P('wide', 'narrow'), may hold values from -6 to 6
- out_grads: bfloat16 [256, 8192], P('wide'), may hold values from -6 to 6
- basis_in: bfloat16 [28672, 28672], P('narrow', 'wide'), may hold values from -0.03125 to 0.03125
- basis_out: bfloat16 [8192, 8192], P('wide', 'narrow'), may hold values from -0.0625 to 0.0625
- eigenvalues: bfloat16 [8192, 28672], P('narrow', 'wide'), may hold values from 0.29882812 to 10
- queries: bfloat16 [2, 8192, 28672], P(None, 'narrow', 'wide'), may hold values from -0.00036621094 to 0.00036621094
- doc_ids: int32 [256], replicated, may hold values from 0 to 15, never falling along the last dimension, each value on 1 to 32 neighbouring positions
Outputs:
- scores: float32 [16, 2], replicated
Inputs may be any that keep to these rules, and one draw needn't show every extreme that they name: `doc_ids`: document numbers never fall along the tokens; each document has 1 to 32 tokens.
All inputs are finite; a program needn't handle non-finite values.
Results may differ from a plain program's by a relative error of at most 0.0051.
Values may be sent and summed in bfloat16 or wider, within the bound.
A program may use at most 192 MiB of HBM per device.

v0:
```python
import functools

import jax
import jax.numpy as jnp
from jax import lax
from jax.experimental import pallas as pl
from jax.experimental.pallas import tpu as pltpu
from jax.sharding import PartitionSpec as P

DOC_PER = 2
DAMPING = 0.1
F32 = jnp.float32
BF16 = jnp.bfloat16
ANY = pl.BlockSpec(memory_space=pl.ANY)
VMEM_LIMIT = 67_043_328


def tile_of(size, most):
    return max(t for t in range(128, most + 1, 128) if size % t == 0)


def grid_of(wide):
    outer = max(o for o in (1, 2, 3, 4) if wide % o == 0)
    return outer, wide // outer


def remote(src, dst, send, recv, device):
    return pltpu.make_async_remote_copy(
        src_ref=src,
        dst_ref=dst,
        send_sem=send,
        recv_sem=recv,
        device_id=device,
        device_id_type=pl.DeviceIdType.MESH,
    )


def greet(wide, narrow):
    w, n = lax.axis_index("wide"), lax.axis_index("narrow")
    barrier = pltpu.get_barrier_semaphore()
    for d in range(1, wide):
        pl.semaphore_signal(
            barrier, inc=1, device_id={"wide": lax.rem(w + d, wide)}, device_id_type=pl.DeviceIdType.MESH
        )
    for d in range(1, narrow):
        pl.semaphore_signal(
            barrier, inc=1, device_id={"narrow": lax.rem(n + d, narrow)}, device_id_type=pl.DeviceIdType.MESH
        )
    pl.semaphore_wait(barrier, wide + narrow - 2)


def score_kernel(
    wide, narrow, docs, acts, grads, basis_in, basis_out, eigenvalues, queries, ids, out,
    acts_all, weights, total, rows_held, weights_out, grads_part, grads_send, first_recv, second_send,
    second_recv, grads_all, acts_send, core_recv, cross_send, cross_recv, acts_done,
    eig_tile, query_tile, mixed, lanes, held, across,
    local_sem, weight_sem, out_sem, eig_sem, query_sem, a2a_s, a2a_r,
    line_s, line_r, side_s, side_r, gline_s, gline_r, gside_s, gside_r,
    first_s, first_r, second_s, second_r, core_s, core_r, cross_s, cross_r, done_s, done_r, last_s, last_r,
    send_w, recv_w, send_n, recv_n,
):
    outer, inner = grid_of(wide)
    cross = narrow // 2
    w, n = lax.axis_index("wide"), lax.axis_index("narrow")
    wo, wi = w // inner, lax.rem(w, inner)
    nx, nc = n // 2, lax.rem(n, 2)
    chunks, tokens, depth = acts_all.shape
    block = acts.shape[0]
    columns = total.shape[1]
    rows_out = basis_out.shape[0]
    half = tokens // 2

    def line_peer(d):
        return {"wide": lax.rem(wo + d, outer) * inner + wi}

    def side_peer(e):
        return {"wide": wo * inner + lax.rem(wi + e, inner)}

    def cut(c):
        return pl.ds(pl.multiple_of(c * depth, 128), depth)

    def rows(source):
        return pl.ds(pl.multiple_of(source * block, block), block)

    def line_source(d):
        return lax.rem(wo + outer - d, outer) * inner + wi

    def weight(c):
        slot = lax.rem(c, 2)
        return pltpu.make_async_copy(
            basis_in.at[pl.ds(pl.multiple_of(c * depth, 128), depth)], weights.at[slot], weight_sem.at[slot]
        )

    fetch_out = pltpu.make_async_copy(basis_out, weights_out, local_sem.at[0])
    own_rows = pltpu.make_async_copy(
        grads.at[:, pl.ds(pl.multiple_of(w * rows_out, 128), rows_out)], rows_held.at[rows(w)], local_sem.at[1]
    )

    def own_acts(c):
        return pltpu.make_async_copy(acts.at[:, cut(c)], acts_all.at[c, rows(w)], out_sem.at[c])

    own_rows.start()
    fetch_out.start()
    for c in range(chunks):
        own_acts(c).start()
    weight(0).start()
    weight(1).start()
    count, width, _ = queries.shape
    jt = eig_tile.shape[2]
    tiles = columns // jt

    def mix_columns(j):
        return pl.ds(pl.multiple_of(j * jt, 128), jt)

    def eig_copy(j):
        slot = lax.rem(j, 2)
        return pltpu.make_async_copy(eigenvalues.at[:, mix_columns(j)], eig_tile.at[slot], eig_sem.at[slot])

    def query_copy(j):
        slot = lax.rem(j, 2)
        return pltpu.make_async_copy(queries.at[:, :, mix_columns(j)], query_tile.at[slot], query_sem.at[slot])

    greet(wide, narrow)

    def swap(d):
        to = lax.rem(w + d, wide)
        return remote(
            grads.at[:, pl.ds(pl.multiple_of(to * rows_out, 128), rows_out)],
            rows_held.at[rows(w)],
            a2a_s.at[d],
            a2a_r.at[d],
            {"wide": to},
        )

    def line_copy(c, d):
        return remote(
            acts.at[:, cut(c)], acts_all.at[c, rows(w)], line_s.at[c, d], line_r.at[c, d], line_peer(d)
        )

    def side_own(c, e):
        return remote(
            acts.at[:, cut(c)], acts_all.at[c, rows(w)], side_s.at[c, e, 0], side_r.at[c, e, 0], side_peer(e)
        )

    def side_pass(c, e, d):
        source = line_source(d)
        return remote(
            acts_all.at[c, rows(source)],
            acts_all.at[c, rows(source)],
            side_s.at[c, e, d],
            side_r.at[c, e, d],
            side_peer(e),
        )

    def begin(c, carry):
        for d in range(1, outer):
            line_copy(c, d).start()
        for e in range(1, inner):
            side_own(c, e).start()
        return carry

    middle = chunks // 2
    for d in range(1, wide):
        swap(d).start()
    lax.fori_loop(0, chunks, begin, 0)
    wt = tile_of(width, 512)

    def grads_tile(k, carry):
        at = pl.ds(pl.multiple_of(k * wt, 128), wt)
        part = jnp.dot(rows_held[...], weights_out[:, at], preferred_element_type=F32)
        part = part.reshape(outer, inner, block, wt)
        grads_part[:, :, :, at] = part
        grads_send[:, :, :, at] = part.astype(BF16)
        return carry

    def first(e):
        return remote(
            grads_send.at[:, lax.rem(wi + e, inner)], first_recv.at[e], first_s.at[e], first_r.at[e], side_peer(e)
        )

    def second(d):
        return remote(
            second_send.at[lax.rem(wo + d, outer)], second_recv.at[d], second_s.at[d], second_r.at[d], line_peer(d)
        )

    ct = tile_of(columns, 512)

    def forward(c):
        for d in range(1, outer):
            line_copy(c, d).wait_recv()
            for e in range(1, inner):
                side_pass(c, e, d).start()

    def step(c, carry):
        @pl.when(c + 1 < chunks)
        def _():
            forward(c + 1)

        own_acts(c).wait()
        for e in range(1, inner):
            side_own(c, e).wait_recv()
            for d in range(1, outer):
                side_pass(c, e, d).wait_recv()
        weight(c).wait()
        slot = lax.rem(c, 2)

        def tile(k, carry):
            at = pl.ds(pl.multiple_of(k * ct, 128), ct)
            part = jnp.dot(acts_all[c], weights[slot, :, at], preferred_element_type=F32)

            @pl.when(c == 0)
            def _():
                total[:, at] = part

            @pl.when(c > 0)
            def _():
                total[:, at] += part

            return carry

        lax.fori_loop(0, columns // ct, tile, 0)

        @pl.when(c + 2 < chunks)
        def _():
            weight(c + 2).start()

        return carry

    own_rows.wait()
    fetch_out.wait()
    for d in range(1, wide):
        swap(d).wait_recv()
    lax.fori_loop(0, width // wt, grads_tile, 0)
    for e in range(1, inner):
        first(e).start()
    forward(0)
    lax.fori_loop(0, middle, step, 0)
    for e in range(1, inner):
        first(e).wait_recv()
    for o in range(outer):
        value = grads_part[o, wi]
        for e in range(1, inner):
            value = value + first_recv[e, o].astype(F32)
        grads_part[o, wi] = value
        second_send[o] = value.astype(BF16)
    for d in range(1, outer):
        second(d).start()
    for j in range(2):
        eig_copy(j).start()
        query_copy(j).start()
    lax.fori_loop(middle, chunks, step, 0)

    share = half // cross

    def to_send(k, carry):
        at = pl.ds(pl.multiple_of(k * ct, 128), ct)
        acts_send[:, at] = total[pl.ds(pl.multiple_of((1 - nc) * half, half), half), at]
        return carry

    lax.fori_loop(0, columns // ct, to_send, 0)
    partner = {"narrow": nx * 2 + (1 - nc)}

    def cross_peer(d):
        return {"narrow": lax.rem(nx + d, cross) * 2 + nc}

    core_copy = remote(acts_send, core_recv, core_s, core_r, partner)
    core_copy.start()

    core_copy.wait_recv()

    def core_sum(k, carry):
        at = pl.ds(pl.multiple_of(k * ct, 128), ct)
        value = total[pl.ds(pl.multiple_of(nc * half, half), half), at] + core_recv[:, at]
        for x in range(cross):
            cross_send[x, :, at] = value[x * share : (x + 1) * share]
        return carry

    lax.fori_loop(0, columns // ct, core_sum, 0)

    def cross_copy(d):
        return remote(
            cross_send.at[lax.rem(nx + d, cross)], cross_recv.at[d], cross_s.at[d], cross_r.at[d], cross_peer(d)
        )

    for d in range(1, cross):
        cross_copy(d).start()

    for d in range(1, outer):
        second(d).wait_recv()
    value = grads_part[wo, wi]
    for d in range(1, outer):
        value = value + second_recv[d].astype(F32)
    grads_all[w] = value.astype(BF16)

    def gline(d):
        return remote(grads_all.at[w], grads_all.at[w], gline_s.at[d], gline_r.at[d], line_peer(d))

    def gside(e, d):
        source = line_source(d)
        return remote(
            grads_all.at[source], grads_all.at[source], gside_s.at[e, d], gside_r.at[e, d], side_peer(e)
        )

    for d in range(1, outer):
        gline(d).start()
    for e in range(1, inner):
        gside(e, 0).start()
    for d in range(1, outer):
        gline(d).wait_recv()
        for e in range(1, inner):
            gside(e, d).start()
    for e in range(1, inner):
        for d in range(outer):
            gside(e, d).wait_recv()

    def mix(j, carry):
        slot = lax.rem(j, 2)
        eig_copy(j).wait()
        query_copy(j).wait()
        left = grads_all[...].reshape(tokens, width)
        scale = 1.0 / (eig_tile[slot].astype(F32) + DAMPING)
        for q in range(count):
            precond = (query_tile[slot, q].astype(F32) * scale).astype(BF16)
            mixed[q, :, mix_columns(j)] = jnp.dot(left, precond, preferred_element_type=F32)

        @pl.when(j + 2 < tiles)
        def _():
            eig_copy(j + 2).start()
            query_copy(j + 2).start()

        return carry

    first_part = tiles // 4
    second_part = (3 * tiles) // 4
    lax.fori_loop(0, first_part, mix, 0)
    for d in range(1, cross):
        cross_copy(d).wait_recv()

    def cross_sum(k, carry):
        at = pl.ds(pl.multiple_of(k * ct, 128), ct)
        value = cross_send[nx, :, at]
        for d in range(1, cross):
            value = value + cross_recv[d, :, at]
        acts_done[nc, nx, :, at] = value.astype(BF16)
        return carry

    lax.fori_loop(0, columns // ct, cross_sum, 0)

    def done_copy(d):
        return remote(acts_done.at[nc, nx], acts_done.at[nc, nx], done_s.at[d], done_r.at[d], cross_peer(d))

    def last_copy(d):
        x = lax.rem(nx + cross - d, cross)
        return remote(acts_done.at[nc, x], acts_done.at[nc, x], last_s.at[d], last_r.at[d], partner)

    for d in range(1, cross):
        done_copy(d).start()
    last_copy(0).start()
    lax.fori_loop(first_part, second_part, mix, 0)
    for d in range(1, cross):
        done_copy(d).wait_recv()
        last_copy(d).start()
    lax.fori_loop(second_part, tiles, mix, 0)
    for d in range(cross):
        last_copy(d).wait_recv()

    lanes[...] = jnp.zeros_like(lanes)

    def fold(j, carry):
        at = pl.ds(pl.multiple_of(j * 128, 128), 128)
        right = acts_done[:, :, :, at].reshape(tokens, 128).astype(F32)
        for q in range(count):
            lanes[q] += mixed[q, :, at] * right
        return carry

    lax.fori_loop(0, columns // 128, fold, 0)
    _, rows_pad, docs_pad = across.shape
    member = (ids[...] == lax.broadcasted_iota(jnp.int32, (docs_pad, tokens), 0)).astype(F32)
    row = lax.broadcasted_iota(jnp.int32, (rows_pad, docs_pad), 0)
    value = jnp.zeros((rows_pad, docs_pad), F32)
    for q in range(count):
        doc_lanes = jnp.dot(member, lanes[q], precision=lax.Precision.HIGHEST, preferred_element_type=F32)
        value = jnp.where(row == q, jnp.sum(doc_lanes, axis=1)[None, :], value)
    across[n] = value

    def over_narrow(d):
        return remote(across.at[n], across.at[n], send_n.at[d], recv_n.at[d], {"narrow": lax.rem(n + d, narrow)})

    def over_wide(d):
        return remote(held.at[w], held.at[w], send_w.at[d], recv_w.at[d], {"wide": lax.rem(w + d, wide)})

    for d in range(1, narrow):
        over_narrow(d).start()
    for d in range(1, narrow):
        over_narrow(d).wait_recv()
    value = across[0]
    for d in range(1, narrow):
        value = value + across[d]
    held[w] = value
    for d in range(1, wide):
        over_wide(d).start()
    for d in range(1, wide):
        over_wide(d).wait_recv()
    value = held[0]
    for d in range(1, wide):
        value = value + held[d]
    out[...] = value[: out.shape[0], : out.shape[1]]

    for d in range(1, wide):
        swap(d).wait_send()

    def drain(c, carry):
        for d in range(1, outer):
            line_copy(c, d).wait_send()
        for e in range(1, inner):
            side_own(c, e).wait_send()
            for d in range(1, outer):
                side_pass(c, e, d).wait_send()
        return carry

    lax.fori_loop(0, chunks, drain, 0)
    for e in range(1, inner):
        first(e).wait_send()
        for d in range(outer):
            gside(e, d).wait_send()
    for d in range(1, outer):
        second(d).wait_send()
        gline(d).wait_send()
    core_copy.wait_send()
    for d in range(1, cross):
        cross_copy(d).wait_send()
        done_copy(d).wait_send()
    for d in range(cross):
        last_copy(d).wait_send()
    for d in range(1, narrow):
        over_narrow(d).wait_send()
    for d in range(1, wide):
        over_wide(d).wait_send()


def score(wide, narrow, activations, out_grads, basis_in, basis_out, eigenvalues, queries, doc_ids):
    outer, inner = grid_of(wide)
    cross = narrow // 2
    block, depth_all = activations.shape
    tokens = block * wide
    docs = DOC_PER * wide
    depth = tile_of(depth_all, 1024)
    chunks = depth_all // depth
    columns = basis_in.shape[1]
    rows_out, width = basis_out.shape
    count = queries.shape[0]
    half = tokens // 2
    jt = tile_of(columns, 256)
    rows_pad, docs_pad = pl.cdiv(count, 8) * 8, pl.cdiv(docs, 128) * 128
    dma = pltpu.SemaphoreType.DMA
    scores = pl.pallas_call(
        functools.partial(score_kernel, wide, narrow, docs),
        out_shape=jax.ShapeDtypeStruct((count, docs), F32),
        in_specs=[ANY] * 6 + [pl.BlockSpec(memory_space=pltpu.VMEM)],
        out_specs=pl.BlockSpec(memory_space=pltpu.VMEM),
        scratch_shapes=[
            pltpu.VMEM((chunks, tokens, depth), BF16),
            pltpu.VMEM((2, depth, columns), BF16),
            pltpu.VMEM((tokens, columns), F32),
            pltpu.VMEM((tokens, rows_out), BF16),
            pltpu.VMEM((rows_out, width), BF16),
            pltpu.VMEM((outer, inner, block, width), F32),
            pltpu.VMEM((outer, inner, block, width), BF16),
            pltpu.VMEM((inner, outer, block, width), BF16),
            pltpu.VMEM((outer, block, width), BF16),
            pltpu.VMEM((outer, block, width), BF16),
            pltpu.VMEM((wide, block, width), BF16),
            pltpu.VMEM((half, columns), F32),
            pltpu.VMEM((half, columns), F32),
            pltpu.VMEM((cross, half // cross, columns), F32),
            pltpu.VMEM((cross, half // cross, columns), F32),
            pltpu.VMEM((2, cross, half // cross, columns), BF16),
            pltpu.VMEM((2, width, jt), BF16),
            pltpu.VMEM((2, count, width, jt), BF16),
            pltpu.VMEM((count, tokens, columns), F32),
            pltpu.VMEM((count, tokens, 128), F32),
            pltpu.VMEM((wide, rows_pad, docs_pad), F32),
            pltpu.VMEM((narrow, rows_pad, docs_pad), F32),
            dma((2,)),
            dma((2,)),
            dma((chunks,)),
            dma((2,)),
            dma((2,)),
            dma((wide,)),
            dma((wide,)),
            dma((chunks, outer)),
            dma((chunks, outer)),
            dma((chunks, inner, outer)),
            dma((chunks, inner, outer)),
            dma((outer,)),
            dma((outer,)),
            dma((inner, outer)),
            dma((inner, outer)),
            dma((inner,)),
            dma((inner,)),
            dma((outer,)),
            dma((outer,)),
            dma,
            dma,
            dma((cross,)),
            dma((cross,)),
            dma((cross,)),
            dma((cross,)),
            dma((cross,)),
            dma((cross,)),
            dma((wide,)),
            dma((wide,)),
            dma((narrow,)),
            dma((narrow,)),
        ],
        compiler_params=pltpu.CompilerParams(
            collective_id=0, has_side_effects=True, vmem_limit_bytes=VMEM_LIMIT
        ),
        name="score",
    )(activations, out_grads, basis_in, basis_out, eigenvalues, queries, doc_ids.reshape(1, tokens))
    return scores.T


def solution(mesh):
    wide, narrow = mesh.shape["wide"], mesh.shape["narrow"]

    def shards(activations, out_grads, basis_in, basis_out, eigenvalues, queries, doc_ids):
        return score(
            wide, narrow, activations, out_grads, basis_in, basis_out, eigenvalues, queries, doc_ids
        )

    return jax.shard_map(
        shards,
        mesh=mesh,
        in_specs=(
            P("wide", "narrow"),
            P("wide", None),
            P("narrow", "wide"),
            P("wide", "narrow"),
            P("narrow", "wide"),
            P(None, "narrow", "wide"),
            P(),
        ),
        out_specs=P(),
        check_vma=False,
    )
```

profile of v0, /device:TPU:0, one launch (start us, length us, event | category | flops | bytes accessed | tf_op | source)
XLA Modules:
  0.0 129.6 jit_solution(1635181325944646840)
XLA Ops:
  0.0 128.4 %score.1 = f32[2,16]{1,0:T(2,128)} custom-call(bf16[32,7168]{1,0:T(8,128)(2,1)} %acts.1, bf16[32,8192]{1,0:T(8,128)(2,1)} %grads.1, bf16[7168,3584]{1,0:T(8,128)(2,1)} %basis_in.1, bf16[1024,2048]{1,0:T(8,128)(2,1)} %basis_out.1, bf16[2048,3584]{1,0:T(8,128)(2,1)} %eigenvalues.1, bf16[2,2048,3584]{2,1,0:T(8,128)(2,1)} %queries.1, s32[1,256]{1,0:T(1,128)} %bitcast.3), custom_call_target="tpu_custom_call" | custom-call | tf_op jit(solution)/shard_map/score/pallas_call | solution.py:456
  128.4 1.2 copy.9
where the time goes:
time: 130 us
  Pallas kernels  128 us (98%)
    pallas_call x1, Pallas kernels, score(): pl.pallas_call(functools.partial(score_kernel, wide, narrow, docs), out_s...  128 us

commit v1 on v0

v1 whole, which is shorter than its diff:
```python
import functools

import jax
import jax.numpy as jnp
from jax import lax
from jax.experimental import pallas as pl
from jax.experimental.pallas import tpu as pltpu
from jax.sharding import PartitionSpec as P

DOC_PER = 2
DAMPING = 0.1
F32 = jnp.float32
BF16 = jnp.bfloat16
ANY = pl.BlockSpec(memory_space=pl.ANY)
VMEM_LIMIT = 67_043_328
PIECES = 8
EARLY = 3


def tile_of(size, most):
    return max(t for t in range(128, most + 1, 128) if size % t == 0)


def grid_of(wide):
    outer = max(o for o in (1, 2, 3, 4) if wide % o == 0)
    return outer, wide // outer


def parts_of(rows_out, narrow):
    return max(p for p in range(1, narrow + 1) if narrow % p == 0 and rows_out % (128 * p) == 0)


def fits(depth, columns, tokens, rows_out, width_out):
    return max(tokens, rows_out) <= depth and width_out + rows_out <= columns


def orders(outer):
    order = []
    for z in range(outer):
        inward = 1 if 2 * z < outer - 1 else -1
        order.append(sorted(range(outer), key=lambda p: (abs(p - z), -inward * (p - z))))
    rank = [[order[z].index(p) for p in range(outer)] for z in range(outer)]
    return order, rank


def lookup(table, i, j):
    value = 0
    for a, row in enumerate(table):
        for b, entry in enumerate(row):
            hit = (i == a) if isinstance(j, int) else jnp.logical_and(i == a, j == b)
            if isinstance(j, int) and b != j:
                continue
            value = value + jnp.where(hit, entry, 0)
    return value


def remote(src, dst, send, recv, device):
    return pltpu.make_async_remote_copy(
        src_ref=src,
        dst_ref=dst,
        send_sem=send,
        recv_sem=recv,
        device_id=device,
        device_id_type=pl.DeviceIdType.MESH,
    )


def greet(wide, narrow):
    w, n = lax.axis_index("wide"), lax.axis_index("narrow")
    barrier = pltpu.get_barrier_semaphore()
    for d in range(1, wide):
        pl.semaphore_signal(
            barrier, inc=1, device_id={"wide": lax.rem(w + d, wide)}, device_id_type=pl.DeviceIdType.MESH
        )
    for d in range(1, narrow):
        pl.semaphore_signal(
            barrier, inc=1, device_id={"narrow": lax.rem(n + d, narrow)}, device_id_type=pl.DeviceIdType.MESH
        )

    def met():
        pl.semaphore_wait(barrier, wide + narrow - 2)

    return met


def score_kernel(
    wide, narrow, docs, acts, grads, basis_in, basis_out, eigenvalues, queries, ids, out,
    pre, basis, acts_all, total, acts_done, core_recv, cross_recv, late_recv,
    rows_spare, weights_spare, grads_own, grads_send, first_recv, second_recv, grads_all, lanes, held, across,
    own_sem, out_sem, eig_sem, query_sem, basis_sem, rows_sem, a2a_s, a2a_r, part_s, part_r,
    up_s, fwd_s, z_r, y_s, y_r, first_s, first_r, second_s, second_r, gz_s, gz_r, gy_s, gy_r,
    core_s, core_r, cross_s, cross_r, late_s, late_r, share_s, share_r, lshare_s, lshare_r,
    send_w, recv_w, send_n, recv_n,
):
    outer, inner = grid_of(wide)
    order, rank = orders(outer)
    cross = narrow // 2
    w, n = lax.axis_index("wide"), lax.axis_index("narrow")
    wo, wi = w // inner, lax.rem(w, inner)
    nx, nc = n // 2, lax.rem(n, 2)
    block, depth_all = acts.shape
    depth, columns = basis.shape[1:]
    chunks = depth_all // depth
    plane = inner * block
    rows_out, width_out = basis_out.shape
    count, width, _ = queries.shape
    slot_plane = [lookup(order, wo, s) for s in range(outer)]

    def side_peer(e):
        return {"wide": wo * inner + lax.rem(wi + e, inner)}

    def line_at(z):
        return {"wide": z * inner + wi}

    def cut(c):
        return pl.ds(pl.multiple_of(c * depth, 128), depth)

    def rows(slot, y):
        return pl.ds(pl.multiple_of(slot * plane + y * block, block), block)

    piece = width // PIECES
    per_slot = depth // piece

    def piece_rows(k, q):
        return pl.ds(pl.multiple_of(q * width + k * piece, 16), piece)

    def eig_rows(k):
        return k // per_slot, pl.ds(pl.multiple_of(lax.rem(k, per_slot) * piece, 16), piece)

    def eig_copy(k):
        slot, at = eig_rows(k)
        return pltpu.make_async_copy(
            eigenvalues.at[pl.ds(pl.multiple_of(k * piece, 16), piece)], basis.at[slot, at], eig_sem.at[k]
        )

    def query_copy(k, q):
        return pltpu.make_async_copy(
            queries.at[q, pl.ds(pl.multiple_of(k * piece, 16), piece)], pre.at[piece_rows(k, q)], query_sem.at[k, q]
        )

    def basis_copy(i):
        slot = lax.rem(i, 3)
        return pltpu.make_async_copy(basis_in.at[cut(lax.rem(i, chunks))], basis.at[slot], basis_sem.at[slot])

    if fits(depth, columns, block * wide, rows_out, width_out):
        weights_out = basis.at[2, pl.ds(0, rows_out), pl.ds(0, width_out)]
        rows_held = basis.at[2, pl.ds(0, block * wide), pl.ds(width_out, rows_out)]
    else:
        weights_out, rows_held = weights_spare, rows_spare
    fetch_out = pltpu.make_async_copy(basis_out, weights_out, out_sem.at[0])

    def own_acts(c):
        return pltpu.make_async_copy(acts.at[:, cut(c)], acts_all.at[rows(0, wi), cut(c)], own_sem.at[c])

    parts = parts_of(rows_out, narrow)
    part, base = lax.rem(n, parts), n // parts * parts
    span = rows_out // parts

    def part_cols(to, p):
        return pl.ds(pl.multiple_of(to * rows_out + p * span, 128), span)

    def held_cols(p):
        return pl.ds(pl.multiple_of(p * span, 128), span)

    def held_rows(source):
        o, i = source // inner, lax.rem(source, inner)
        return pl.ds(pl.multiple_of((i * outer + o) * block, block), block)

    own_rows = pltpu.make_async_copy(
        grads.at[:, part_cols(w, part)], rows_held.at[held_rows(w), held_cols(part)], rows_sem.at[0]
    )

    met = greet(wide, narrow)
    own_rows.start()
    for k in range(EARLY + 1):
        eig_copy(k).start()
        for q in range(count):
            query_copy(k, q).start()
    fetch_out.start()
    for c in range(chunks):
        own_acts(c).start()
    for k in range(EARLY + 1, PIECES):
        eig_copy(k).start()
        for q in range(count):
            query_copy(k, q).start()

    strip = 32

    def precondition(k):
        eig_copy(k).wait()
        for q in range(count):
            query_copy(k, q).wait()
        slot = k // per_slot
        start = lax.rem(k, per_slot) * piece

        def strip_of(r, carry):
            at = pl.ds(pl.multiple_of(start + r * strip, strip), strip)
            scale = 1.0 / (basis[slot, at].astype(F32) + DAMPING)
            for q in range(count):
                here = pl.ds(pl.multiple_of(q * width + k * piece + r * strip, strip), strip)
                pre[here] = (pre[here].astype(F32) * scale).astype(BF16)
            return carry

        lax.fori_loop(0, piece // strip, strip_of, 0)

    for k in range(EARLY):
        precondition(k)
    met()

    def swap(d):
        to = lax.rem(w + d, wide)
        return remote(
            grads.at[:, part_cols(to, part)], rows_held.at[held_rows(w), held_cols(part)],
            a2a_s.at[d], a2a_r.at[d], {"wide": to},
        )

    def part_copy(j):
        return remote(
            rows_held.at[:, held_cols(part)], rows_held.at[:, held_cols(part)],
            part_s.at[j], part_r.at[j], {"narrow": base + lax.rem(part + j, parts)},
        )

    def own_line(c, up):
        to = wo + 1 if up else wo - 1
        slot = lookup(rank, to, wo)
        return remote(
            acts.at[:, cut(c)], acts_all.at[rows(slot, wi), cut(c)], up_s.at[int(up), c], z_r.at[slot, c], line_at(to)
        )

    def line_wait(s, c):
        return remote(
            acts.at[:, cut(c)], acts_all.at[rows(s, wi), cut(c)], fwd_s.at[s, c], z_r.at[s, c], line_at(wo)
        )

    def onward(s):
        above = slot_plane[s] > wo
        to = jnp.where(above, wo - 1, wo + 1)
        return to, jnp.logical_and(to >= 0, to < outer)

    def forward(s, c):
        to, _ = onward(s)
        slot = lookup(rank, to, slot_plane[s])
        return remote(
            acts_all.at[rows(s, wi), cut(c)], acts_all.at[rows(slot, wi), cut(c)],
            fwd_s.at[s, c], z_r.at[slot, c], line_at(to),
        )

    def side_copy(e, s, c):
        source = acts.at[:, cut(c)] if s == 0 else acts_all.at[rows(s, wi), cut(c)]
        return remote(source, acts_all.at[rows(s, wi), cut(c)], y_s.at[e, s, c], y_r.at[e, s, c], side_peer(e))

    def relay(s, c):
        line_wait(s, c).wait_recv()
        _, more = onward(s)

        @pl.when(more)
        def _():
            forward(s, c).start()

        for e in range(1, inner):
            side_copy(e, s, c).start()

    for d in range(1, wide):
        swap(d).start()

    def begin(c, carry):
        for e in range(1, inner):
            side_copy(e, 0, c).start()

        @pl.when(wo + 1 < outer)
        def _():
            own_line(c, True).start()

        @pl.when(wo > 0)
        def _():
            own_line(c, False).start()

        return carry

    lax.fori_loop(0, chunks, begin, 0)

    per_turn = pl.cdiv(PIECES - EARLY, chunks)

    def turn_one(c, carry):
        for j in range(per_turn):
            k = EARLY + c * per_turn + j

            @pl.when(k < PIECES)
            def _():
                precondition(k)

            @pl.when(k == min(per_slot, PIECES) - 1)
            def _():
                basis_copy(0).start()

            @pl.when(k == PIECES - 1)
            def _():
                basis_copy(1).start()

        relay(1, c)

        @pl.when(c == min(1, chunks - 1))
        def _():
            own_rows.wait()
            for d in range(1, wide):
                swap(d).wait_recv()
            for j in range(1, parts):
                part_copy(j).start()

        return carry

    lax.fori_loop(0, chunks, turn_one, 0)

    fetch_out.wait()
    for j in range(1, parts):
        part_copy(j).wait_recv()
    wt = tile_of(width_out, 512)

    def grads_tile(k, carry):
        at = pl.ds(pl.multiple_of(k * wt, 128), wt)
        right = weights_out[:, at]

        def left(i):
            return rows_held[pl.ds(pl.multiple_of(i * outer * block, block), outer * block), :]

        own = jnp.dot(left(wi), right, preferred_element_type=F32)
        grads_own[:, :, at] = own.reshape(outer, block, wt)
        for e in range(1, inner):
            i = lax.rem(wi + e, inner)
            other = jnp.dot(left(i), right, preferred_element_type=F32).astype(BF16)
            grads_send[i, :, :, at] = other.reshape(outer, block, wt)
        return carry

    lax.fori_loop(0, width_out // wt, grads_tile, 0)
    for j in range(1, parts):
        part_copy(j).wait_send()
    basis_copy(2).start()

    def first(e):
        return remote(
            grads_send.at[lax.rem(wi + e, inner)], first_recv.at[e - 1], first_s.at[e], first_r.at[e], side_peer(e)
        )

    def second(d):
        to = lax.rem(wo + d, outer)
        return remote(
            grads_send.at[wi, to], second_recv.at[d - 1], second_s.at[d], second_r.at[d], line_at(to)
        )

    for e in range(1, inner):
        first(e).start()

    pair = 2 * plane
    ct = tile_of(columns, 1792)

    def rotate(g, c):
        i = g * chunks + c
        basis_copy(i).wait()
        slot = lax.rem(i, 3)

        def tile(k, carry):
            at = pl.ds(pl.multiple_of(k * ct, 128), ct)
            value = jnp.dot(
                acts_all[g * pair : (g + 1) * pair, cut(c)], basis[slot, :, at], preferred_element_type=F32
            )

            @pl.when(c == 0)
            def _():
                total[:, at] = value

            @pl.when(c > 0)
            def _():
                total[:, at] += value

            return carry

        lax.fori_loop(0, columns // ct, tile, 0)

        @pl.when(i + 3 < 2 * chunks)
        def _():
            basis_copy(i + 3).start()

    def turn_two(c, carry):
        own_acts(c).wait()
        for e in range(1, inner):
            side_copy(e, 0, c).wait_recv()
        relay(2, c)
        for e in range(1, inner):
            side_copy(e, 1, c).wait_recv()
        rotate(0, c)
        return carry

    lax.fori_loop(0, chunks, turn_two, 0)

    partner = {"narrow": nx * 2 + (1 - nc)}
    mine = pl.ds(pl.multiple_of(nc * plane, plane), plane)
    theirs = pl.ds(pl.multiple_of((1 - nc) * plane, plane), plane)
    cols = 4 if columns % 512 == 0 else 1
    cw = columns // cols

    def lane(k):
        return pl.ds(pl.multiple_of(k * cw, 128), cw)

    def cross_peer(d):
        return {"narrow": lax.rem(nx + d, cross) * 2 + nc}

    def core_copy(g):
        return remote(total.at[theirs], core_recv, core_s.at[g], core_r.at[g], partner)

    def cross_copy(d):
        return remote(total.at[mine], cross_recv.at[d - 1], cross_s.at[d], cross_r.at[d], cross_peer(d))

    def done_rows(g):
        return pl.ds(pl.multiple_of((2 * g + nc) * plane, plane), plane)

    def share_copy():
        return remote(
            acts_done.at[done_rows(0)], acts_done.at[done_rows(0)], share_s.at[0], share_r.at[0], partner
        )

    def late_copy(d, k):
        return remote(
            acts_done.at[done_rows(1), lane(k)], late_recv.at[d - 1, :, lane(k)], late_s.at[d, k], late_r.at[d, k], cross_peer(d)
        )

    def late_share(k):
        here = acts_done.at[done_rows(1), lane(k)]
        return remote(here, here, lshare_s.at[k], lshare_r.at[k], partner)

    core_copy(0).start()
    core_copy(0).wait_recv()

    def core_sum(k, carry):
        total[mine, lane(k)] += core_recv[:, lane(k)]
        return carry

    lax.fori_loop(0, cols, core_sum, 0)
    for d in range(1, cross):
        cross_copy(d).start()

    def turn_three(c, carry):
        relay(3, c)
        return carry

    lax.fori_loop(0, chunks, turn_three, 0)

    for e in range(1, inner):
        first(e).wait_recv()
    for o in range(outer):
        value = grads_own[o]
        for e in range(1, inner):
            value = value + first_recv[e - 1, o].astype(F32)
        grads_own[o] = value
        grads_send[wi, o] = value.astype(BF16)
    for d in range(1, outer):
        second(d).start()

    def group_done():
        for d in range(1, cross):
            cross_copy(d).wait_recv()

        def cross_sum(k, carry):
            value = total[mine, lane(k)]
            for d in range(1, cross):
                value = value + cross_recv[d - 1, :, lane(k)]
            acts_done[done_rows(0), lane(k)] = value.astype(BF16)
            return carry

        lax.fori_loop(0, cols, cross_sum, 0)
        share_copy().start()

    for d in range(1, outer):
        second(d).wait_recv()
    value = grads_own[wo]
    for d in range(1, outer):
        value = value + second_recv[d - 1].astype(F32)
    grads_all[0, wi] = value.astype(BF16)

    def gline(d):
        to = lax.rem(wo + d, outer)
        slot = lookup(rank, to, wo)
        return remote(grads_all.at[0, wi], grads_all.at[slot, wi], gz_s.at[d], gz_r.at[slot], line_at(to))

    def gline_wait(s):
        return remote(grads_all.at[0, wi], grads_all.at[s, wi], gz_s.at[s], gz_r.at[s], line_at(wo))

    def gside(e, s):
        return remote(
            grads_all.at[s, wi], grads_all.at[s, wi], gy_s.at[e, s], gy_r.at[e, s], side_peer(e)
        )

    for d in range(1, outer):
        gline(d).start()
    for e in range(1, inner):
        gside(e, 0).start()

    group_done()
    core_copy(0).wait_send()
    for d in range(1, cross):
        cross_copy(d).wait_send()

    def turn_four(c, carry):
        for s in (2, 3):
            for e in range(1, inner):
                side_copy(e, s, c).wait_recv()
        rotate(1, c)
        return carry

    lax.fori_loop(0, chunks, turn_four, 0)
    share_copy().wait_recv()
    core_copy(1).start()
    for s in range(1, outer):
        gline_wait(s).wait_recv()
        for e in range(1, inner):
            gside(e, s).start()
    core_copy(1).wait_recv()

    def late_sum(k, carry):
        value = total[mine, lane(k)] + core_recv[:, lane(k)]
        total[mine, lane(k)] = value
        acts_done[done_rows(1), lane(k)] = value.astype(BF16)
        for d in range(1, cross):
            late_copy(d, k).start()
        return carry

    lax.fori_loop(0, cols, late_sum, 0)

    lanes[...] = jnp.zeros_like(lanes)

    def mix(g, k):
        left = grads_all[2 * g : 2 * g + 2].reshape(pair, width)
        here = slice(g * pair, (g + 1) * pair)
        for q in range(count):
            mixed = jnp.dot(left, pre[q * width : (q + 1) * width, lane(k)], preferred_element_type=F32)
            right = acts_done[here, lane(k)].astype(F32)
            value = lanes[q, here]
            for j in range(cw // 128):
                value = value + mixed[:, j * 128 : (j + 1) * 128] * right[:, j * 128 : (j + 1) * 128]
            lanes[q, here] = value

    for e in range(1, inner):
        for s in (0, 1):
            gside(e, s).wait_recv()

    def mix_early(k, carry):
        mix(0, k)
        return carry

    lax.fori_loop(0, cols, mix_early, 0)
    for e in range(1, inner):
        for s in (2, 3):
            gside(e, s).wait_recv()

    def late_done(k):
        for d in range(1, cross):
            late_copy(d, k).wait()
        value = total[mine, lane(k)]
        for d in range(1, cross):
            value = value + late_recv[d - 1, :, lane(k)].astype(F32)
        acts_done[done_rows(1), lane(k)] = value.astype(BF16)
        late_share(k).start()

    late_done(0)

    def mix_late(k, carry):
        @pl.when(k + 1 < cols)
        def _():
            late_done(k + 1)

        late_share(k).wait_recv()
        mix(1, k)
        return carry

    lax.fori_loop(0, cols, mix_late, 0)

    _, rows_pad, docs_pad = across.shape
    row = lax.broadcasted_iota(jnp.int32, (rows_pad, docs_pad), 0)
    value = jnp.zeros((rows_pad, docs_pad), F32)
    members = [
        (ids[slot_plane[s]] == lax.broadcasted_iota(jnp.int32, (docs_pad, plane), 0)).astype(F32)
        for s in range(outer)
    ]
    for q in range(count):
        doc_lanes = jnp.zeros((docs_pad, 128), F32)
        for s in range(outer):
            doc_lanes = doc_lanes + jnp.dot(
                members[s],
                lanes[q, s * plane : (s + 1) * plane],
                precision=lax.Precision.HIGHEST,
                preferred_element_type=F32,
            )
        value = jnp.where(row == q, jnp.sum(doc_lanes, axis=1)[None, :], value)
    across[n] = value

    def over_narrow(d):
        return remote(across.at[n], across.at[n], send_n.at[d], recv_n.at[d], {"narrow": lax.rem(n + d, narrow)})

    def over_wide(d):
        return remote(held.at[w], held.at[w], send_w.at[d], recv_w.at[d], {"wide": lax.rem(w + d, wide)})

    for d in range(1, narrow):
        over_narrow(d).start()
    for d in range(1, narrow):
        over_narrow(d).wait_recv()
    value = across[0]
    for d in range(1, narrow):
        value = value + across[d]
    held[w] = value
    for d in range(1, wide):
        over_wide(d).start()
    for d in range(1, wide):
        over_wide(d).wait_recv()
    value = held[0]
    for d in range(1, wide):
        value = value + held[d]
    out[...] = value[: out.shape[0], : out.shape[1]]

    for d in range(1, wide):
        swap(d).wait_send()

    def drain(c, carry):
        @pl.when(wo + 1 < outer)
        def _():
            own_line(c, True).wait_send()

        @pl.when(wo > 0)
        def _():
            own_line(c, False).wait_send()

        for s in range(1, outer):
            _, more = onward(s)

            @pl.when(more)
            def _():
                forward(s, c).wait_send()

        for s in range(outer):
            for e in range(1, inner):
                side_copy(e, s, c).wait_send()
        return carry

    lax.fori_loop(0, chunks, drain, 0)
    for e in range(1, inner):
        first(e).wait_send()
        for s in range(outer):
            gside(e, s).wait_send()
    for d in range(1, outer):
        second(d).wait_send()
        gline(d).wait_send()
    core_copy(1).wait_send()
    share_copy().wait_send()
    for k in range(cols):
        late_share(k).wait_send()
    for d in range(1, narrow):
        over_narrow(d).wait_send()
    for d in range(1, wide):
        over_wide(d).wait_send()


def score(wide, narrow, activations, out_grads, basis_in, basis_out, eigenvalues, queries, doc_ids):
    outer, inner = grid_of(wide)
    cross = narrow // 2
    block, depth_all = activations.shape
    tokens = block * wide
    plane = block * inner
    docs = DOC_PER * wide
    depth = tile_of(depth_all, 1024)
    chunks = depth_all // depth
    columns = basis_in.shape[1]
    rows_out, width_out = basis_out.shape
    count, width, _ = queries.shape
    cols = 4 if columns % 512 == 0 else 1
    parts = parts_of(rows_out, narrow)
    inside = fits(depth, columns, tokens, rows_out, width_out)
    rows_pad, docs_pad = pl.cdiv(count, 8) * 8, pl.cdiv(docs, 128) * 128
    dma = pltpu.SemaphoreType.DMA
    scores = pl.pallas_call(
        functools.partial(score_kernel, wide, narrow, docs),
        out_shape=jax.ShapeDtypeStruct((count, docs), F32),
        in_specs=[ANY] * 6 + [pl.BlockSpec(memory_space=pltpu.VMEM)],
        out_specs=pl.BlockSpec(memory_space=pltpu.VMEM),
        scratch_shapes=[
            pltpu.VMEM((count * width, columns), BF16),
            pltpu.VMEM((3, depth, columns), BF16),
            pltpu.VMEM((tokens, depth_all), BF16),
            pltpu.VMEM((2 * plane, columns), F32),
            pltpu.VMEM((tokens, columns), BF16),
            pltpu.VMEM((plane, columns), F32),
            pltpu.VMEM((cross - 1, plane, columns), F32),
            pltpu.VMEM((cross - 1, plane, columns), BF16),
            pltpu.VMEM((16, 128) if inside else (tokens, rows_out), BF16),
            pltpu.VMEM((16, 128) if inside else (rows_out, width_out), BF16),
            pltpu.VMEM((outer, block, width_out), F32),
            pltpu.VMEM((inner, outer, block, width_out), BF16),
            pltpu.VMEM((inner - 1, outer, block, width_out), BF16),
            pltpu.VMEM((outer - 1, block, width_out), BF16),
            pltpu.VMEM((outer, inner, block, width_out), BF16),
            pltpu.VMEM((count, tokens, 128), F32),
            pltpu.VMEM((wide, rows_pad, docs_pad), F32),
            pltpu.VMEM((narrow, rows_pad, docs_pad), F32),
            dma((chunks,)),
            dma((1,)),
            dma((PIECES,)),
            dma((PIECES, count)),
            dma((3,)),
            dma((1,)),
            dma((wide,)),
            dma((wide,)),
            dma((parts,)),
            dma((parts,)),
            dma((2, chunks)),
            dma((outer, chunks)),
            dma((outer, chunks)),
            dma((inner, outer, chunks)),
            dma((inner, outer, chunks)),
            dma((inner,)),
            dma((inner,)),
            dma((outer,)),
            dma((outer,)),
            dma((outer,)),
            dma((outer,)),
            dma((inner, outer)),
            dma((inner, outer)),
            dma((2,)),
            dma((2,)),
            dma((cross,)),
            dma((cross,)),
            dma((cross, cols)),
            dma((cross, cols)),
            dma((1,)),
            dma((1,)),
            dma((cols,)),
            dma((cols,)),
            dma((wide,)),
            dma((wide,)),
            dma((narrow,)),
            dma((narrow,)),
        ],
        compiler_params=pltpu.CompilerParams(
            collective_id=0, has_side_effects=True, vmem_limit_bytes=VMEM_LIMIT
        ),
        name="score",
    )(activations, out_grads, basis_in, basis_out, eigenvalues, queries, doc_ids.reshape(outer, 1, plane))
    return scores.T


def solution(mesh):
    wide, narrow = mesh.shape["wide"], mesh.shape["narrow"]

    def shards(activations, out_grads, basis_in, basis_out, eigenvalues, queries, doc_ids):
        return score(
            wide, narrow, activations, out_grads, basis_in, basis_out, eigenvalues, queries, doc_ids
        )

    return jax.shard_map(
        shards,
        mesh=mesh,
        in_specs=(
            P("wide", "narrow"),
            P("wide", None),
            P("narrow", "wide"),
            P("wide", "narrow"),
            P("narrow", "wide"),
            P(None, "narrow", "wide"),
            P(),
        ),
        out_specs=P(),
        check_vma=False,
    )
```

time: 130 us -> 116 us (0.89)
  Pallas kernels: 128 us -> 113 us
  local copies, waits for them, and re-layouts: 1.24 us -> 2.57 us
    pallas_call x1, Pallas kernels: 128 us -> 113 us  [score(): pl.pallas_call(functools.partial(score_kernel, wide, narrow, docs), out_s...]
    reshape x0 -> x1, local copies, waits for them, and re-layouts: none -> 1.35 us  [score(): doc_ids.reshape(outer, 1, plane)]
where the time goes in v1:
time: 116 us; the launch traced here: 115 us
  Pallas kernels  113 us (97%)
  local copies, waits for them, and re-layouts  2.57 us (2%)
    pallas_call x1, Pallas kernels, score(): pl.pallas_call(functools.partial(score_kernel, wide, narrow, docs), out_s...  113 us

profile of v1, /device:TPU:0, one launch (start us, length us, event | category | flops | bytes accessed | tf_op | source)
XLA Modules:
  0.0 115.3 jit_solution(13296991549440669158)
XLA Ops:
  0.0 1.4 %reshape.3.ids = s32[4,1,64]{2,1,0:T(1,128)} reshape(s32[256]{0:T(256)} %param.13) | data formatting | bytes 2048 | tf_op jit(solution)/shard_map/reshape | solution.py:743
  1.4 112.7 %score.1 = f32[2,16]{1,0:T(2,128)} custom-call(bf16[32,7168]{1,0:T(8,128)(2,1)} %acts.1, bf16[32,8192]{1,0:T(8,128)(2,1)} %grads.1, bf16[7168,3584]{1,0:T(8,128)(2,1)} %basis_in.1, bf16[1024,2048]{1,0:T(8,128)(2,1)} %basis_out.1, bf16[2048,3584]{1,0:T(8,128)(2,1)} %eigenvalues.1, bf16[2,2048,3584]{2,1,0:T(8,128)(2,1)} %queries.1, s32[4,1,64]{2,1,0:T(1,128)} %reshape.3.ids), custom_call_target="tpu_custom_call" | custom-call | tf_op jit(solution)/shard_map/score/pallas_call | solution.py:677
  114.1 1.2 %copy.9 = f32[16,2]{0,1:T(2,128)} copy(f32[16,2]{0,1:T(2,128)} %bitcast.1) | data formatting | bytes 256

commit v2 on v1

--- a/solution.py
+++ b/solution.py
@@ -13,8 +13,9 @@
 BF16 = jnp.bfloat16
 ANY = pl.BlockSpec(memory_space=pl.ANY)
 VMEM_LIMIT = 67_043_328
-PIECES = 8
-EARLY = 3
+PIECES = 16
+EARLY = 2
+AHEAD = 4
 
 
 def tile_of(size, most):
@@ -130,12 +131,14 @@
     def eig_copy(k):
         slot, at = eig_rows(k)
         return pltpu.make_async_copy(
-            eigenvalues.at[pl.ds(pl.multiple_of(k * piece, 16), piece)], basis.at[slot, at], eig_sem.at[k]
+            eigenvalues.at[pl.ds(pl.multiple_of(k * piece, 16), piece)], basis.at[slot, at], eig_sem.at[lax.rem(k, AHEAD)]
         )
 
     def query_copy(k, q):
         return pltpu.make_async_copy(
-            queries.at[q, pl.ds(pl.multiple_of(k * piece, 16), piece)], pre.at[piece_rows(k, q)], query_sem.at[k, q]
+            queries.at[q, pl.ds(pl.multiple_of(k * piece, 16), piece)],
+            pre.at[piece_rows(k, q)],
+            query_sem.at[lax.rem(k, AHEAD), q],
         )
 
     def basis_copy(i):
@@ -149,8 +152,7 @@
         weights_out, rows_held = weights_spare, rows_spare
     fetch_out = pltpu.make_async_copy(basis_out, weights_out, out_sem.at[0])
 
-    def own_acts(c):
-        return pltpu.make_async_copy(acts.at[:, cut(c)], acts_all.at[rows(0, wi), cut(c)], own_sem.at[c])
+    own_acts = pltpu.make_async_copy(acts, acts_all.at[rows(0, wi)], own_sem.at[0])
 
     parts = parts_of(rows_out, narrow)
     part, base = lax.rem(n, parts), n // parts * parts
@@ -172,21 +174,22 @@
 
     met = greet(wide, narrow)
     own_rows.start()
-    for k in range(EARLY + 1):
+
+    def fetch_piece(k):
         eig_copy(k).start()
         for q in range(count):
             query_copy(k, q).start()
-    fetch_out.start()
-    for c in range(chunks):
-        own_acts(c).start()
-    for k in range(EARLY + 1, PIECES):
-        eig_copy(k).start()
-        for q in range(count):
-            query_copy(k, q).start()
+
+    for k in range(AHEAD - 1):
+        fetch_piece(k)
 
     strip = 32
 
     def precondition(k):
+        @pl.when(k + AHEAD - 1 < PIECES)
+        def _():
+            fetch_piece(k + AHEAD - 1)
+
         eig_copy(k).wait()
         for q in range(count):
             query_copy(k, q).wait()
@@ -211,7 +214,7 @@
         to = lax.rem(w + d, wide)
         return remote(
             grads.at[:, part_cols(to, part)], rows_held.at[held_rows(w), held_cols(part)],
-            a2a_s.at[d], a2a_r.at[d], {"wide": to},
+            a2a_s.at[0], a2a_r.at[d], {"wide": to},
         )
 
     def part_copy(j):
@@ -224,12 +227,12 @@
         to = wo + 1 if up else wo - 1
         slot = lookup(rank, to, wo)
         return remote(
-            acts.at[:, cut(c)], acts_all.at[rows(slot, wi), cut(c)], up_s.at[int(up), c], z_r.at[slot, c], line_at(to)
+            acts.at[:, cut(c)], acts_all.at[rows(slot, wi), cut(c)], up_s.at[int(up)], z_r.at[slot, c], line_at(to)
         )
 
     def line_wait(s, c):
         return remote(
-            acts.at[:, cut(c)], acts_all.at[rows(s, wi), cut(c)], fwd_s.at[s, c], z_r.at[s, c], line_at(wo)
+            acts.at[:, cut(c)], acts_all.at[rows(s, wi), cut(c)], fwd_s.at[s], z_r.at[s, c], line_at(wo)
         )
 
     def onward(s):
@@ -242,14 +245,16 @@
         slot = lookup(rank, to, slot_plane[s])
         return remote(
             acts_all.at[rows(s, wi), cut(c)], acts_all.at[rows(slot, wi), cut(c)],
-            fwd_s.at[s, c], z_r.at[slot, c], line_at(to),
+            fwd_s.at[s], z_r.at[slot, c], line_at(to),
         )
 
     def side_copy(e, s, c):
         source = acts.at[:, cut(c)] if s == 0 else acts_all.at[rows(s, wi), cut(c)]
-        return remote(source, acts_all.at[rows(s, wi), cut(c)], y_s.at[e, s, c], y_r.at[e, s, c], side_peer(e))
-
-    def relay(s, c):
+        return remote(source, acts_all.at[rows(s, wi), cut(c)], y_s.at[e - 1, s], y_r.at[e - 1, s, c], side_peer(e))
+
+    amid = jnp.logical_and(wo > 0, wo < outer - 1)
+
+    def arrive(s, c):
         line_wait(s, c).wait_recv()
         _, more = onward(s)
 
@@ -257,6 +262,7 @@
         def _():
             forward(s, c).start()
 
+    def across_side(s, c):
         for e in range(1, inner):
             side_copy(e, s, c).start()
 
@@ -297,7 +303,17 @@
             def _():
                 basis_copy(1).start()
 
-        relay(1, c)
+        arrive(1, c)
+        across_side(1, c)
+
+        @pl.when(amid)
+        def _():
+            arrive(2, c)
+
+        @pl.when(c == 0)
+        def _():
+            fetch_out.start()
+            own_acts.start()
 
         @pl.when(c == min(1, chunks - 1))
         def _():
@@ -381,21 +397,30 @@
             basis_copy(i + 3).start()
 
     def turn_two(c, carry):
-        own_acts(c).wait()
+        @pl.when(jnp.logical_not(amid))
+        def _():
+            arrive(2, c)
+
+        across_side(2, c)
+
+        @pl.when(amid)
+        def _():
+            arrive(3, c)
+
         for e in range(1, inner):
             side_copy(e, 0, c).wait_recv()
-        relay(2, c)
         for e in range(1, inner):
             side_copy(e, 1, c).wait_recv()
         rotate(0, c)
         return carry
 
+    own_acts.wait()
     lax.fori_loop(0, chunks, turn_two, 0)
 
     partner = {"narrow": nx * 2 + (1 - nc)}
     mine = pl.ds(pl.multiple_of(nc * plane, plane), plane)
     theirs = pl.ds(pl.multiple_of((1 - nc) * plane, plane), plane)
-    cols = 4 if columns % 512 == 0 else 1
+    cols = 7 if columns % 896 == 0 else 1
     cw = columns // cols
 
     def lane(k):
@@ -408,7 +433,7 @@
         return remote(total.at[theirs], core_recv, core_s.at[g], core_r.at[g], partner)
 
     def cross_copy(d):
-        return remote(total.at[mine], cross_recv.at[d - 1], cross_s.at[d], cross_r.at[d], cross_peer(d))
+        return remote(core_recv, cross_recv.at[d - 1], cross_s.at[d], cross_r.at[d], cross_peer(d))
 
     def done_rows(g):
         return pl.ds(pl.multiple_of((2 * g + nc) * plane, plane), plane)
@@ -431,7 +456,7 @@
     core_copy(0).wait_recv()
 
     def core_sum(k, carry):
-        total[mine, lane(k)] += core_recv[:, lane(k)]
+        core_recv[:, lane(k)] += total[mine, lane(k)]
         return carry
 
     lax.fori_loop(0, cols, core_sum, 0)
@@ -439,7 +464,11 @@
         cross_copy(d).start()
 
     def turn_three(c, carry):
-        relay(3, c)
+        @pl.when(jnp.logical_not(amid))
+        def _():
+            arrive(3, c)
+
+        across_side(3, c)
         return carry
 
     lax.fori_loop(0, chunks, turn_three, 0)
@@ -457,10 +486,10 @@
 
     def group_done():
         for d in range(1, cross):
-            cross_copy(d).wait_recv()
+            cross_copy(d).wait()
 
         def cross_sum(k, carry):
-            value = total[mine, lane(k)]
+            value = core_recv[:, lane(k)]
             for d in range(1, cross):
                 value = value + cross_recv[d - 1, :, lane(k)]
             acts_done[done_rows(0), lane(k)] = value.astype(BF16)
@@ -469,13 +498,6 @@
         lax.fori_loop(0, cols, cross_sum, 0)
         share_copy().start()
 
-    for d in range(1, outer):
-        second(d).wait_recv()
-    value = grads_own[wo]
-    for d in range(1, outer):
-        value = value + second_recv[d - 1].astype(F32)
-    grads_all[0, wi] = value.astype(BF16)
-
     def gline(d):
         to = lax.rem(wo + d, outer)
         slot = lookup(rank, to, wo)
@@ -489,30 +511,44 @@
             grads_all.at[s, wi], grads_all.at[s, wi], gy_s.at[e, s], gy_r.at[e, s], side_peer(e)
         )
 
-    for d in range(1, outer):
-        gline(d).start()
-    for e in range(1, inner):
-        gside(e, 0).start()
-
-    group_done()
     core_copy(0).wait_send()
-    for d in range(1, cross):
-        cross_copy(d).wait_send()
 
     def turn_four(c, carry):
         for s in (2, 3):
             for e in range(1, inner):
                 side_copy(e, s, c).wait_recv()
         rotate(1, c)
+
+        @pl.when(c == chunks // 2)
+        def _():
+            for d in range(1, outer):
+                second(d).wait_recv()
+            value = grads_own[wo]
+            for d in range(1, outer):
+                value = value + second_recv[d - 1].astype(F32)
+            grads_all[0, wi] = value.astype(BF16)
+
+            for d in range(1, outer):
+                gline(d).start()
+            for e in range(1, inner):
+                gside(e, 0).start()
+
+        @pl.when(c == chunks - 2)
+        def _():
+            group_done()
+
         return carry
 
     lax.fori_loop(0, chunks, turn_four, 0)
     share_copy().wait_recv()
     core_copy(1).start()
-    for s in range(1, outer):
+
+    def grads_across(s):
         gline_wait(s).wait_recv()
         for e in range(1, inner):
             gside(e, s).start()
+
+    grads_across(1)
     core_copy(1).wait_recv()
 
     def late_sum(k, carry):
@@ -524,6 +560,8 @@
         return carry
 
     lax.fori_loop(0, cols, late_sum, 0)
+    for s in range(2, outer):
+        grads_across(s)
 
     lanes[...] = jnp.zeros_like(lanes)
 
@@ -533,10 +571,12 @@
         for q in range(count):
             mixed = jnp.dot(left, pre[q * width : (q + 1) * width, lane(k)], preferred_element_type=F32)
             right = acts_done[here, lane(k)].astype(F32)
-            value = lanes[q, here]
+            value = jnp.zeros((pair, 128), F32)
             for j in range(cw // 128):
                 value = value + mixed[:, j * 128 : (j + 1) * 128] * right[:, j * 128 : (j + 1) * 128]
-            lanes[q, here] = value
+            for h in range(2):
+                there = pl.ds(pl.multiple_of(slot_plane[2 * g + h] * plane, plane), plane)
+                lanes[q, there] += value[h * plane : (h + 1) * plane]
 
     for e in range(1, inner):
         for s in (0, 1):
@@ -576,27 +616,19 @@
     _, rows_pad, docs_pad = across.shape
     row = lax.broadcasted_iota(jnp.int32, (rows_pad, docs_pad), 0)
     value = jnp.zeros((rows_pad, docs_pad), F32)
-    members = [
-        (ids[slot_plane[s]] == lax.broadcasted_iota(jnp.int32, (docs_pad, plane), 0)).astype(F32)
-        for s in range(outer)
-    ]
+    tokens = block * wide
+    named = jnp.broadcast_to(ids[...].reshape(1, tokens), (docs_pad, tokens))
+    member = (named == lax.broadcasted_iota(jnp.int32, (docs_pad, tokens), 0)).astype(F32)
     for q in range(count):
-        doc_lanes = jnp.zeros((docs_pad, 128), F32)
-        for s in range(outer):
-            doc_lanes = doc_lanes + jnp.dot(
-                members[s],
-                lanes[q, s * plane : (s + 1) * plane],
-                precision=lax.Precision.HIGHEST,
-                preferred_element_type=F32,
-            )
+        doc_lanes = jnp.dot(member, lanes[q], precision=lax.Precision.HIGHEST, preferred_element_type=F32)
         value = jnp.where(row == q, jnp.sum(doc_lanes, axis=1)[None, :], value)
     across[n] = value
 
     def over_narrow(d):
-        return remote(across.at[n], across.at[n], send_n.at[d], recv_n.at[d], {"narrow": lax.rem(n + d, narrow)})
+        return remote(across.at[n], across.at[n], send_n.at[0], recv_n.at[d], {"narrow": lax.rem(n + d, narrow)})
 
     def over_wide(d):
-        return remote(held.at[w], held.at[w], send_w.at[d], recv_w.at[d], {"wide": lax.rem(w + d, wide)})
+        return remote(held.at[w], held.at[w], send_w.at[0], recv_w.at[d], {"wide": lax.rem(w + d, wide)})
 
     for d in range(1, narrow):
         over_narrow(d).start()
@@ -615,31 +647,30 @@
         value = value + held[d]
     out[...] = value[: out.shape[0], : out.shape[1]]
 
-    for d in range(1, wide):
-        swap(d).wait_send()
-
-    def drain(c, carry):
-        @pl.when(wo + 1 < outer)
-        def _():
-            own_line(c, True).wait_send()
-
-        @pl.when(wo > 0)
-        def _():
-            own_line(c, False).wait_send()
-
-        for s in range(1, outer):
-            _, more = onward(s)
-
-            @pl.when(more)
-            def _():
-                forward(s, c).wait_send()
-
-        for s in range(outer):
-            for e in range(1, inner):
-                side_copy(e, s, c).wait_send()
-        return carry
-
-    lax.fori_loop(0, chunks, drain, 0)
+    def left(source, sem):
+        pltpu.make_async_copy(source, source, sem).wait()
+
+    left(rows_held.at[pl.ds(0, (wide - 1) * block), held_cols(0)], a2a_s.at[0])
+    row_block = acts_all.at[rows(0, wi)]
+
+    @pl.when(wo + 1 < outer)
+    def _():
+        left(row_block, up_s.at[1])
+
+    @pl.when(wo > 0)
+    def _():
+        left(row_block, up_s.at[0])
+
+    for s in range(1, outer):
+        _, more = onward(s)
+
+        @pl.when(more)
+        def _():
+            left(row_block, fwd_s.at[s])
+
+    for s in range(outer):
+        for e in range(1, inner):
+            left(row_block, y_s.at[e - 1, s])
     for e in range(1, inner):
         first(e).wait_send()
         for s in range(outer):
@@ -651,10 +682,8 @@
     share_copy().wait_send()
     for k in range(cols):
         late_share(k).wait_send()
-    for d in range(1, narrow):
-        over_narrow(d).wait_send()
-    for d in range(1, wide):
-        over_wide(d).wait_send()
+    left(across.at[pl.ds(0, narrow - 1)], send_n.at[0])
+    left(held.at[pl.ds(0, wide - 1)], send_w.at[0])
 
 
 def score(wide, narrow, activations, out_grads, basis_in, basis_out, eigenvalues, queries, doc_ids):
@@ -669,7 +698,7 @@
     columns = basis_in.shape[1]
     rows_out, width_out = basis_out.shape
     count, width, _ = queries.shape
-    cols = 4 if columns % 512 == 0 else 1
+    cols = 7 if columns % 896 == 0 else 1
     parts = parts_of(rows_out, narrow)
     inside = fits(depth, columns, tokens, rows_out, width_out)
     rows_pad, docs_pad = pl.cdiv(count, 8) * 8, pl.cdiv(docs, 128) * 128
@@ -698,49 +727,49 @@
             pltpu.VMEM((count, tokens, 128), F32),
             pltpu.VMEM((wide, rows_pad, docs_pad), F32),
             pltpu.VMEM((narrow, rows_pad, docs_pad), F32),
-            dma((chunks,)),
             dma((1,)),
-            dma((PIECES,)),
-            dma((PIECES, count)),
+            dma((1,)),
+            dma((AHEAD,)),
+            dma((AHEAD, count,)),
             dma((3,)),
             dma((1,)),
-            dma((wide,)),
+            dma((1,)),
             dma((wide,)),
             dma((parts,)),
             dma((parts,)),
-            dma((2, chunks)),
-            dma((outer, chunks)),
-            dma((outer, chunks)),
-            dma((inner, outer, chunks)),
-            dma((inner, outer, chunks)),
+            dma((2,)),
+            dma((outer,)),
+            dma((outer, chunks,)),
+            dma((inner - 1, outer,)),
+            dma((inner - 1, outer, chunks,)),
             dma((inner,)),
             dma((inner,)),
             dma((outer,)),
             dma((outer,)),
             dma((outer,)),
             dma((outer,)),
-            dma((inner, outer)),
-            dma((inner, outer)),
+            dma((inner, outer,)),
+            dma((inner, outer,)),
             dma((2,)),
             dma((2,)),
             dma((cross,)),
             dma((cross,)),
-            dma((cross, cols)),
-            dma((cross, cols)),
+            dma((cross, cols,)),
+            dma((cross, cols,)),
             dma((1,)),
             dma((1,)),
             dma((cols,)),
             dma((cols,)),
+            dma((1,)),
             dma((wide,)),
-            dma((wide,)),
-            dma((narrow,)),
+            dma((1,)),
             dma((narrow,)),
         ],
         compiler_params=pltpu.CompilerParams(
             collective_id=0, has_side_effects=True, vmem_limit_bytes=VMEM_LIMIT
         ),
         name="score",
-    )(activations, out_grads, basis_in, basis_out, eigenvalues, queries, doc_ids.reshape(outer, 1, plane))
+    )(activations, out_grads, basis_in, basis_out, eigenvalues, queries, doc_ids)
     return scores.T
 
 

time: 116 us -> 98.8 us (0.85)
  Pallas kernels: 113 us -> 97.4 us
  local copies, waits for them, and re-layouts: 2.57 us -> 1.24 us
    pallas_call x1, Pallas kernels: 113 us -> 97.4 us  [score(): pl.pallas_call(functools.partial(score_kernel, wide, narrow, docs), out_s...]
    reshape x1 -> x0, local copies, waits for them, and re-layouts: 1.35 us -> none  [score(): doc_ids.reshape(outer, 1, plane)]
where the time goes in v2:
time: 98.8 us; the launch traced here: 98.7 us
  Pallas kernels  97.4 us (99%)
  local copies, waits for them, and re-layouts  1.24 us (1%)
    pallas_call x1, Pallas kernels, score(): pl.pallas_call(functools.partial(score_kernel, wide, narrow, docs), out_s...  97.4 us

profile of v2, /device:TPU:0, one launch (start us, length us, event | category | flops | bytes accessed | tf_op | source)
XLA Modules:
  0.0 98.7 jit_solution(12354544555273154077)
XLA Ops:
  0.0 97.4 %score.1 = f32[2,16]{1,0:T(2,128)} custom-call(bf16[32,7168]{1,0:T(8,128)(2,1)} %acts.1, bf16[32,8192]{1,0:T(8,128)(2,1)} %grads.1, bf16[7168,3584]{1,0:T(8,128)(2,1)} %basis_in.1, bf16[1024,2048]{1,0:T(8,128)(2,1)} %basis_out.1, bf16[2048,3584]{1,0:T(8,128)(2,1)} %eigenvalues.1, bf16[2,2048,3584]{2,1,0:T(8,128)(2,1)} %queries.1, s32[256]{0:T(256)} %ids.1), custom_call_target="tpu_custom_call" | custom-call | tf_op jit(solution)/shard_map/score/pallas_call | solution.py:706
  97.4 1.2 %copy.9 = f32[16,2]{0,1:T(2,128)} copy(f32[16,2]{0,1:T(2,128)} %bitcast.1) | data formatting | bytes 256

commit v3 on v2

--- a/solution.py
+++ b/solution.py
@@ -14,8 +14,10 @@
 ANY = pl.BlockSpec(memory_space=pl.ANY)
 VMEM_LIMIT = 67_043_328
 PIECES = 16
-EARLY = 2
+EARLY = 1
+BEFORE = 4
 AHEAD = 4
+DETOUR = 4
 
 
 def tile_of(size, most):
@@ -89,8 +91,8 @@
     pre, basis, acts_all, total, acts_done, core_recv, cross_recv, late_recv,
     rows_spare, weights_spare, grads_own, grads_send, first_recv, second_recv, grads_all, lanes, held, across,
     own_sem, out_sem, eig_sem, query_sem, basis_sem, rows_sem, a2a_s, a2a_r, part_s, part_r,
-    up_s, fwd_s, z_r, y_s, y_r, first_s, first_r, second_s, second_r, gz_s, gz_r, gy_s, gy_r,
-    core_s, core_r, cross_s, cross_r, late_s, late_r, share_s, share_r, lshare_s, lshare_r,
+    up_s, fwd_s, z_r, x_s, x_r, y_s, y_r, first_s, first_r, second_s, second_r, gz_s, gz_r, gy_s, gy_r,
+    core_s, core_r, cross_s, cross_r, late_s, late_r, done_s, done_r, share_s, share_r, lshare_s, lshare_r,
     send_w, recv_w, send_n, recv_n,
 ):
     outer, inner = grid_of(wide)
@@ -120,13 +122,12 @@
         return pl.ds(pl.multiple_of(slot * plane + y * block, block), block)
 
     piece = width // PIECES
-    per_slot = depth // piece
 
     def piece_rows(k, q):
         return pl.ds(pl.multiple_of(q * width + k * piece, 16), piece)
 
     def eig_rows(k):
-        return k // per_slot, pl.ds(pl.multiple_of(lax.rem(k, per_slot) * piece, 16), piece)
+        return 1, pl.ds(pl.multiple_of(lax.rem(k, AHEAD) * piece, 16), piece)
 
     def eig_copy(k):
         slot, at = eig_rows(k)
@@ -193,8 +194,7 @@
         eig_copy(k).wait()
         for q in range(count):
             query_copy(k, q).wait()
-        slot = k // per_slot
-        start = lax.rem(k, per_slot) * piece
+        slot, start = 1, lax.rem(k, AHEAD) * piece
 
         def strip_of(r, carry):
             at = pl.ds(pl.multiple_of(start + r * strip, strip), strip)
@@ -252,6 +252,7 @@
         source = acts.at[:, cut(c)] if s == 0 else acts_all.at[rows(s, wi), cut(c)]
         return remote(source, acts_all.at[rows(s, wi), cut(c)], y_s.at[e - 1, s], y_r.at[e - 1, s, c], side_peer(e))
 
+    bent = DETOUR if inner == 2 else 0
     amid = jnp.logical_and(wo > 0, wo < outer - 1)
 
     def arrive(s, c):
@@ -262,6 +263,23 @@
         def _():
             forward(s, c).start()
 
+    other = 1 - wi
+
+    def detour(s, c):
+        if s == 0:
+            to, source = jnp.where(wo == 0, 1, outer - 2), wo
+        else:
+            (to, _), source = onward(s), slot_plane[s]
+        slot = lookup(rank, to, source)
+        return remote(
+            acts_all.at[rows(s, other), cut(c)], acts_all.at[rows(slot, other), cut(c)],
+            x_s.at[s], x_r.at[slot, c], line_at(to),
+        )
+
+    def detour_wait(s, c):
+        here = acts_all.at[rows(s, other), cut(c)]
+        remote(here, here, x_s.at[s], x_r.at[s, c], line_at(wo)).wait_recv()
+
     def across_side(s, c):
         for e in range(1, inner):
             side_copy(e, s, c).start()
@@ -285,51 +303,6 @@
 
     lax.fori_loop(0, chunks, begin, 0)
 
-    per_turn = pl.cdiv(PIECES - EARLY, chunks)
-
-    def turn_one(c, carry):
-        for j in range(per_turn):
-            k = EARLY + c * per_turn + j
-
-            @pl.when(k < PIECES)
-            def _():
-                precondition(k)
-
-            @pl.when(k == min(per_slot, PIECES) - 1)
-            def _():
-                basis_copy(0).start()
-
-            @pl.when(k == PIECES - 1)
-            def _():
-                basis_copy(1).start()
-
-        arrive(1, c)
-        across_side(1, c)
-
-        @pl.when(amid)
-        def _():
-            arrive(2, c)
-
-        @pl.when(c == 0)
-        def _():
-            fetch_out.start()
-            own_acts.start()
-
-        @pl.when(c == min(1, chunks - 1))
-        def _():
-            own_rows.wait()
-            for d in range(1, wide):
-                swap(d).wait_recv()
-            for j in range(1, parts):
-                part_copy(j).start()
-
-        return carry
-
-    lax.fori_loop(0, chunks, turn_one, 0)
-
-    fetch_out.wait()
-    for j in range(1, parts):
-        part_copy(j).wait_recv()
     wt = tile_of(width_out, 512)
 
     def grads_tile(k, carry):
@@ -347,11 +320,6 @@
             grads_send[i, :, :, at] = other.reshape(outer, block, wt)
         return carry
 
-    lax.fori_loop(0, width_out // wt, grads_tile, 0)
-    for j in range(1, parts):
-        part_copy(j).wait_send()
-    basis_copy(2).start()
-
     def first(e):
         return remote(
             grads_send.at[lax.rem(wi + e, inner)], first_recv.at[e - 1], first_s.at[e], first_r.at[e], side_peer(e)
@@ -363,6 +331,69 @@
             grads_send.at[wi, to], second_recv.at[d - 1], second_s.at[d], second_r.at[d], line_at(to)
         )
 
+    def partial_grads():
+        fetch_out.wait()
+        for j in range(1, parts):
+            part_copy(j).wait_recv()
+        lax.fori_loop(0, width_out // wt, grads_tile, 0)
+        for j in range(1, parts):
+            part_copy(j).wait_send()
+        basis_copy(2).start()
+
+    for k in range(EARLY, BEFORE):
+        precondition(k)
+    per_turn = pl.cdiv(PIECES - BEFORE, chunks - 1)
+
+    def turn_one(c, carry):
+        for j in range(per_turn):
+            k = BEFORE + c * per_turn + j
+
+            @pl.when(k < PIECES)
+            def _():
+                precondition(k)
+
+            @pl.when(k == PIECES - AHEAD + 1)
+            def _():
+                basis_copy(0).start()
+
+            @pl.when(k == PIECES - 1)
+            def _():
+                basis_copy(1).start()
+
+        arrive(1, c)
+        across_side(1, c)
+
+        @pl.when(amid)
+        def _():
+            arrive(2, c)
+
+        @pl.when(c == 0)
+        def _():
+            fetch_out.start()
+            own_acts.start()
+
+        if bent:
+
+            @pl.when(jnp.logical_and(jnp.logical_not(amid), c < bent))
+            def _():
+                side_copy(1, 0, c).wait_recv()
+                detour(0, c).start()
+
+        @pl.when(c == max(chunks - 5, 0))
+        def _():
+            own_rows.wait()
+            for d in range(1, wide):
+                swap(d).wait_recv()
+            for j in range(1, parts):
+                part_copy(j).start()
+
+        @pl.when(c == chunks - 2)
+        def _():
+            partial_grads()
+
+        return carry
+
+    lax.fori_loop(0, chunks, turn_one, 0)
     for e in range(1, inner):
         first(e).start()
 
@@ -396,19 +427,49 @@
         def _():
             basis_copy(i + 3).start()
 
+    def relay_two(c):
+        @pl.when(jnp.logical_not(amid))
+        def _():
+            arrive(2, c)
+
+        straight = jnp.logical_not(jnp.logical_and(amid, c < bent))
+
+        @pl.when(straight)
+        def _():
+            across_side(2, c)
+
+        @pl.when(amid)
+        def _():
+            arrive(3, c)
+
+        if bent:
+
+            @pl.when(jnp.logical_not(straight))
+            def _():
+                detour_wait(2, c)
+                detour(2, c).start()
+
     def turn_two(c, carry):
-        @pl.when(jnp.logical_not(amid))
-        def _():
-            arrive(2, c)
-
-        across_side(2, c)
-
-        @pl.when(amid)
-        def _():
-            arrive(3, c)
-
-        for e in range(1, inner):
-            side_copy(e, 0, c).wait_recv()
+        for j in range(2):
+            ahead = 2 * c + j
+
+            @pl.when(ahead < chunks)
+            def _():
+                relay_two(ahead)
+
+        @pl.when(jnp.logical_or(amid, c >= bent))
+        def _():
+            for e in range(1, inner):
+                side_copy(e, 0, c).wait_recv()
+
+        if bent:
+            late = c - (chunks - bent)
+
+            @pl.when(jnp.logical_and(amid, late >= 0))
+            def _():
+                detour_wait(3, late)
+                detour(3, late).start()
+
         for e in range(1, inner):
             side_copy(e, 1, c).wait_recv()
         rotate(0, c)
@@ -422,6 +483,7 @@
     theirs = pl.ds(pl.multiple_of((1 - nc) * plane, plane), plane)
     cols = 7 if columns % 896 == 0 else 1
     cw = columns // cols
+    share = plane // cross
 
     def lane(k):
         return pl.ds(pl.multiple_of(k * cw, 128), cw)
@@ -433,15 +495,25 @@
         return remote(total.at[theirs], core_recv, core_s.at[g], core_r.at[g], partner)
 
     def cross_copy(d):
-        return remote(core_recv, cross_recv.at[d - 1], cross_s.at[d], cross_r.at[d], cross_peer(d))
+        to = lax.rem(nx + d, cross)
+        return remote(
+            core_recv.at[pl.ds(pl.multiple_of(to * share, share), share)],
+            cross_recv.at[d - 1], cross_s.at[d], cross_r.at[d], cross_peer(d),
+        )
 
     def done_rows(g):
         return pl.ds(pl.multiple_of((2 * g + nc) * plane, plane), plane)
 
-    def share_copy():
-        return remote(
-            acts_done.at[done_rows(0)], acts_done.at[done_rows(0)], share_s.at[0], share_r.at[0], partner
-        )
+    def share_rows(x):
+        return pl.ds(pl.multiple_of(nc * plane + x * share, share), share)
+
+    def done_copy(d):
+        here = acts_done.at[share_rows(nx)]
+        return remote(here, here, done_s.at[d], done_r.at[d], cross_peer(d))
+
+    def last_copy(d):
+        here = acts_done.at[share_rows(lax.rem(nx + cross - d, cross))]
+        return remote(here, here, share_s.at[d], share_r.at[d], partner)
 
     def late_copy(d, k):
         return remote(
@@ -468,7 +540,10 @@
         def _():
             arrive(3, c)
 
-        across_side(3, c)
+        @pl.when(c >= bent)
+        def _():
+            across_side(3, c)
+
         return carry
 
     lax.fori_loop(0, chunks, turn_three, 0)
@@ -484,19 +559,27 @@
     for d in range(1, outer):
         second(d).start()
 
+    def group_shares():
+        for d in range(1, cross):
+            cross_copy(d).wait()
+        here = pl.ds(pl.multiple_of(nx * share, share), share)
+
+        def cross_sum(k, carry):
+            value = core_recv[here, lane(k)]
+            for d in range(1, cross):
+                value = value + cross_recv[d - 1, :, lane(k)]
+            acts_done[share_rows(nx), lane(k)] = value.astype(BF16)
+            return carry
+
+        lax.fori_loop(0, cols, cross_sum, 0)
+        for d in range(1, cross):
+            done_copy(d).start()
+        last_copy(0).start()
+
     def group_done():
         for d in range(1, cross):
-            cross_copy(d).wait()
-
-        def cross_sum(k, carry):
-            value = core_recv[:, lane(k)]
-            for d in range(1, cross):
-                value = value + cross_recv[d - 1, :, lane(k)]
-            acts_done[done_rows(0), lane(k)] = value.astype(BF16)
-            return carry
-
-        lax.fori_loop(0, cols, cross_sum, 0)
-        share_copy().start()
+            done_copy(d).wait_recv()
+            last_copy(d).start()
 
     def gline(d):
         to = lax.rem(wo + d, outer)
@@ -513,34 +596,51 @@
 
     core_copy(0).wait_send()
 
+    def grads_done():
+        for d in range(1, outer):
+            second(d).wait_recv()
+        value = grads_own[wo]
+        for d in range(1, outer):
+            value = value + second_recv[d - 1].astype(F32)
+        grads_all[0, wi] = value.astype(BF16)
+
+        for d in range(1, outer):
+            gline(d).start()
+        for e in range(1, inner):
+            gside(e, 0).start()
+
     def turn_four(c, carry):
-        for s in (2, 3):
+        @pl.when(jnp.logical_not(jnp.logical_and(amid, c < bent)))
+        def _():
             for e in range(1, inner):
-                side_copy(e, s, c).wait_recv()
+                side_copy(e, 2, c).wait_recv()
+
+        @pl.when(c >= bent)
+        def _():
+            for e in range(1, inner):
+                side_copy(e, 3, c).wait_recv()
+
+        if bent:
+
+            @pl.when(jnp.logical_and(jnp.logical_not(amid), c < bent))
+            def _():
+                detour_wait(3, c)
+
         rotate(1, c)
 
-        @pl.when(c == chunks // 2)
-        def _():
-            for d in range(1, outer):
-                second(d).wait_recv()
-            value = grads_own[wo]
-            for d in range(1, outer):
-                value = value + second_recv[d - 1].astype(F32)
-            grads_all[0, wi] = value.astype(BF16)
-
-            for d in range(1, outer):
-                gline(d).start()
-            for e in range(1, inner):
-                gside(e, 0).start()
-
-        @pl.when(c == chunks - 2)
-        def _():
-            group_done()
+        @pl.when(c == jnp.where(amid, chunks // 2 + 1, chunks // 2 - 1))
+        def _():
+            group_shares()
+
+        @pl.when(c == jnp.where(amid, chunks // 2 + 1, chunks - 2))
+        def _():
+            grads_done()
 
         return carry
 
     lax.fori_loop(0, chunks, turn_four, 0)
-    share_copy().wait_recv()
+    group_done()
+    last_copy(0).wait_recv()
     core_copy(1).start()
 
     def grads_across(s):
@@ -548,7 +648,6 @@
         for e in range(1, inner):
             gside(e, s).start()
 
-    grads_across(1)
     core_copy(1).wait_recv()
 
     def late_sum(k, carry):
@@ -560,7 +659,7 @@
         return carry
 
     lax.fori_loop(0, cols, late_sum, 0)
-    for s in range(2, outer):
+    for s in range(1, outer):
         grads_across(s)
 
     lanes[...] = jnp.zeros_like(lanes)
@@ -578,6 +677,8 @@
                 there = pl.ds(pl.multiple_of(slot_plane[2 * g + h] * plane, plane), plane)
                 lanes[q, there] += value[h * plane : (h + 1) * plane]
 
+    for d in range(1, cross):
+        last_copy(d).wait_recv()
     for e in range(1, inner):
         for s in (0, 1):
             gside(e, s).wait_recv()
@@ -587,9 +688,6 @@
         return carry
 
     lax.fori_loop(0, cols, mix_early, 0)
-    for e in range(1, inner):
-        for s in (2, 3):
-            gside(e, s).wait_recv()
 
     def late_done(k):
         for d in range(1, cross):
@@ -600,13 +698,16 @@
         acts_done[done_rows(1), lane(k)] = value.astype(BF16)
         late_share(k).start()
 
-    late_done(0)
+    def late_turn(k, carry):
+        late_done(k)
+        return carry
+
+    lax.fori_loop(0, cols, late_turn, 0)
+    for e in range(1, inner):
+        for s in (2, 3):
+            gside(e, s).wait_recv()
 
     def mix_late(k, carry):
-        @pl.when(k + 1 < cols)
-        def _():
-            late_done(k + 1)
-
         late_share(k).wait_recv()
         mix(1, k)
         return carry
@@ -668,9 +769,32 @@
         def _():
             left(row_block, fwd_s.at[s])
 
-    for s in range(outer):
-        for e in range(1, inner):
+    for e in range(1, inner):
+        for s in (0, 1):
             left(row_block, y_s.at[e - 1, s])
+        short = acts_all.at[rows(0, wi), pl.ds(0, (chunks - bent) * depth)]
+        left(short, y_s.at[e - 1, 3])
+
+        @pl.when(amid)
+        def _():
+            left(short, y_s.at[e - 1, 2])
+
+        @pl.when(jnp.logical_not(amid))
+        def _():
+            left(row_block, y_s.at[e - 1, 2])
+
+    if bent:
+        long = acts_all.at[rows(0, wi), pl.ds(0, bent * depth)]
+
+        @pl.when(amid)
+        def _():
+            left(long, x_s.at[2])
+            left(long, x_s.at[3])
+
+        @pl.when(jnp.logical_not(amid))
+        def _():
+            left(long, x_s.at[0])
+
     for e in range(1, inner):
         first(e).wait_send()
         for s in range(outer):
@@ -679,7 +803,10 @@
         second(d).wait_send()
         gline(d).wait_send()
     core_copy(1).wait_send()
-    share_copy().wait_send()
+    for d in range(cross):
+        last_copy(d).wait_send()
+    for d in range(1, cross):
+        done_copy(d).wait_send()
     for k in range(cols):
         late_share(k).wait_send()
     left(across.at[pl.ds(0, narrow - 1)], send_n.at[0])
@@ -715,7 +842,7 @@
             pltpu.VMEM((2 * plane, columns), F32),
             pltpu.VMEM((tokens, columns), BF16),
             pltpu.VMEM((plane, columns), F32),
-            pltpu.VMEM((cross - 1, plane, columns), F32),
+            pltpu.VMEM((cross - 1, plane // cross, columns), F32),
             pltpu.VMEM((cross - 1, plane, columns), BF16),
             pltpu.VMEM((16, 128) if inside else (tokens, rows_out), BF16),
             pltpu.VMEM((16, 128) if inside else (rows_out, width_out), BF16),
@@ -739,7 +866,9 @@
             dma((parts,)),
             dma((2,)),
             dma((outer,)),
-            dma((outer, chunks,)),
+            dma((outer, chunks)),
+            dma((outer,)),
+            dma((outer, max(DETOUR, 1))),
             dma((inner - 1, outer,)),
             dma((inner - 1, outer, chunks,)),
             dma((inner,)),
@@ -756,8 +885,10 @@
             dma((cross,)),
             dma((cross, cols,)),
             dma((cross, cols,)),
-            dma((1,)),
-            dma((1,)),
+            dma((cross,)),
+            dma((cross,)),
+            dma((cross,)),
+            dma((cross,)),
             dma((cols,)),
             dma((cols,)),
             dma((1,)),

time: 98.8 us -> 92.9 us (0.940)
  Pallas kernels: 97.4 us -> 91.5 us
    pallas_call x1, Pallas kernels: 97.4 us -> 91.5 us  [score(): pl.pallas_call(functools.partial(score_kernel, wide, narrow, docs), out_s...]
where the time goes in v3:
time: 92.9 us; the launch traced here: 92.7 us
  Pallas kernels  91.5 us (98%)
  local copies, waits for them, and re-layouts  1.24 us (1%)
    pallas_call x1, Pallas kernels, score(): pl.pallas_call(functools.partial(score_kernel, wide, narrow, docs), out_s...  91.5 us

profile of v3, /device:TPU:0, one launch (start us, length us, event | category | flops | bytes accessed | tf_op | source)
XLA Modules:
  0.0 92.7 jit_solution(16190888977424266066)
XLA Ops:
  0.0 91.5 %score.1 = f32[2,16]{1,0:T(2,128)} custom-call(bf16[32,7168]{1,0:T(8,128)(2,1)} %acts.1, bf16[32,8192]{1,0:T(8,128)(2,1)} %grads.1, bf16[7168,3584]{1,0:T(8,128)(2,1)} %basis_in.1, bf16[1024,2048]{1,0:T(8,128)(2,1)} %basis_out.1, bf16[2048,3584]{1,0:T(8,128)(2,1)} %eigenvalues.1, bf16[2,2048,3584]{2,1,0:T(8,128)(2,1)} %queries.1, s32[256]{0:T(256)} %ids.1), custom_call_target="tpu_custom_call" | custom-call | tf_op jit(solution)/shard_map/score/pallas_call | solution.py:833
  91.5 1.2 %copy.9 = f32[16,2]{0,1:T(2,128)} copy(f32[16,2]{0,1:T(2,128)} %bitcast.1) | data formatting | bytes 256

commit v4 on v3

--- a/solution.py
+++ b/solution.py
@@ -17,7 +17,7 @@
 EARLY = 1
 BEFORE = 4
 AHEAD = 4
-DETOUR = 4
+DETOUR = 3
 
 
 def tile_of(size, most):
@@ -88,11 +88,11 @@
 
 def score_kernel(
     wide, narrow, docs, acts, grads, basis_in, basis_out, eigenvalues, queries, ids, out,
-    pre, basis, acts_all, total, acts_done, core_recv, cross_recv, late_recv,
+    pre, basis, acts_all, total, acts_done, core_recv, cross_recv,
     rows_spare, weights_spare, grads_own, grads_send, first_recv, second_recv, grads_all, lanes, held, across,
     own_sem, out_sem, eig_sem, query_sem, basis_sem, rows_sem, a2a_s, a2a_r, part_s, part_r,
     up_s, fwd_s, z_r, x_s, x_r, y_s, y_r, first_s, first_r, second_s, second_r, gz_s, gz_r, gy_s, gy_r,
-    core_s, core_r, cross_s, cross_r, late_s, late_r, done_s, done_r, share_s, share_r, lshare_s, lshare_r,
+    core_s, core_r, cross_s, cross_r, late_s, late_r, spread_s, spread_r, done_s, done_r, share_s, share_r, lshare_s, lshare_r,
     send_w, recv_w, send_n, recv_n,
 ):
     outer, inner = grid_of(wide)
@@ -173,6 +173,9 @@
         grads.at[:, part_cols(w, part)], rows_held.at[held_rows(w), held_cols(part)], rows_sem.at[0]
     )
 
+    def left(source, sem):
+        pltpu.make_async_copy(source, source, sem).wait()
+
     met = greet(wide, narrow)
     own_rows.start()
 
@@ -220,7 +223,7 @@
     def part_copy(j):
         return remote(
             rows_held.at[:, held_cols(part)], rows_held.at[:, held_cols(part)],
-            part_s.at[j], part_r.at[j], {"narrow": base + lax.rem(part + j, parts)},
+            part_s.at[0], part_r.at[j - 1], {"narrow": base + lax.rem(part + j, parts)},
         )
 
     def own_line(c, up):
@@ -273,12 +276,12 @@
         slot = lookup(rank, to, source)
         return remote(
             acts_all.at[rows(s, other), cut(c)], acts_all.at[rows(slot, other), cut(c)],
-            x_s.at[s], x_r.at[slot, c], line_at(to),
+            x_s.at[s], x_r.at[slot - 2, c], line_at(to),
         )
 
     def detour_wait(s, c):
         here = acts_all.at[rows(s, other), cut(c)]
-        remote(here, here, x_s.at[s], x_r.at[s, c], line_at(wo)).wait_recv()
+        remote(here, here, x_s.at[s], x_r.at[s - 2, c], line_at(wo)).wait_recv()
 
     def across_side(s, c):
         for e in range(1, inner):
@@ -328,7 +331,7 @@
     def second(d):
         to = lax.rem(wo + d, outer)
         return remote(
-            grads_send.at[wi, to], second_recv.at[d - 1], second_s.at[d], second_r.at[d], line_at(to)
+            grads_send.at[wi, to], second_recv.at[d - 1], second_s.at[0], second_r.at[d - 1], line_at(to)
         )
 
     def partial_grads():
@@ -336,8 +339,7 @@
         for j in range(1, parts):
             part_copy(j).wait_recv()
         lax.fori_loop(0, width_out // wt, grads_tile, 0)
-        for j in range(1, parts):
-            part_copy(j).wait_send()
+        left(rows_held.at[:, pl.ds(0, (parts - 1) * span)], part_s.at[0])
         basis_copy(2).start()
 
     for k in range(EARLY, BEFORE):
@@ -501,9 +503,6 @@
             cross_recv.at[d - 1], cross_s.at[d], cross_r.at[d], cross_peer(d),
         )
 
-    def done_rows(g):
-        return pl.ds(pl.multiple_of((2 * g + nc) * plane, plane), plane)
-
     def share_rows(x):
         return pl.ds(pl.multiple_of(nc * plane + x * share, share), share)
 
@@ -515,14 +514,25 @@
         here = acts_done.at[share_rows(lax.rem(nx + cross - d, cross))]
         return remote(here, here, share_s.at[d], share_r.at[d], partner)
 
+    def part_of(x):
+        return pl.ds(pl.multiple_of(nc * plane + x * share, share), share)
+
+    def late_rows(x):
+        return pl.ds(pl.multiple_of((2 + nc) * plane + x * share, share), share)
+
     def late_copy(d, k):
         return remote(
-            acts_done.at[done_rows(1), lane(k)], late_recv.at[d - 1, :, lane(k)], late_s.at[d, k], late_r.at[d, k], cross_peer(d)
-        )
-
-    def late_share(k):
-        here = acts_done.at[done_rows(1), lane(k)]
-        return remote(here, here, lshare_s.at[k], lshare_r.at[k], partner)
+            total.at[part_of(lax.rem(nx + d, cross)), lane(k)], cross_recv.at[d - 1, :, lane(k)],
+            late_s.at[d - 1], late_r.at[d - 1, k], cross_peer(d),
+        )
+
+    def late_spread(d, k):
+        here = acts_done.at[late_rows(nx), lane(k)]
+        return remote(here, here, spread_s.at[d - 1], spread_r.at[d - 1, k], cross_peer(d))
+
+    def late_share(d, k):
+        here = acts_done.at[late_rows(lax.rem(nx + cross - d, cross)), lane(k)]
+        return remote(here, here, lshare_s.at[d], lshare_r.at[d, k], partner)
 
     core_copy(0).start()
     core_copy(0).wait_recv()
@@ -584,14 +594,14 @@
     def gline(d):
         to = lax.rem(wo + d, outer)
         slot = lookup(rank, to, wo)
-        return remote(grads_all.at[0, wi], grads_all.at[slot, wi], gz_s.at[d], gz_r.at[slot], line_at(to))
+        return remote(grads_all.at[0, wi], grads_all.at[slot, wi], gz_s.at[0], gz_r.at[slot], line_at(to))
 
     def gline_wait(s):
-        return remote(grads_all.at[0, wi], grads_all.at[s, wi], gz_s.at[s], gz_r.at[s], line_at(wo))
+        return remote(grads_all.at[0, wi], grads_all.at[s, wi], gz_s.at[0], gz_r.at[s], line_at(wo))
 
     def gside(e, s):
         return remote(
-            grads_all.at[s, wi], grads_all.at[s, wi], gy_s.at[e, s], gy_r.at[e, s], side_peer(e)
+            grads_all.at[s, wi], grads_all.at[s, wi], gy_s.at[e - 1], gy_r.at[e - 1, s], side_peer(e)
         )
 
     core_copy(0).wait_send()
@@ -653,7 +663,6 @@
     def late_sum(k, carry):
         value = total[mine, lane(k)] + core_recv[:, lane(k)]
         total[mine, lane(k)] = value
-        acts_done[done_rows(1), lane(k)] = value.astype(BF16)
         for d in range(1, cross):
             late_copy(d, k).start()
         return carry
@@ -677,6 +686,28 @@
                 there = pl.ds(pl.multiple_of(slot_plane[2 * g + h] * plane, plane), plane)
                 lanes[q, there] += value[h * plane : (h + 1) * plane]
 
+    def late_add(k):
+        for d in range(1, cross):
+            late_copy(d, k).wait_recv()
+        value = total[part_of(nx), lane(k)]
+        for d in range(1, cross):
+            value = value + cross_recv[d - 1, :, lane(k)]
+        acts_done[late_rows(nx), lane(k)] = value.astype(BF16)
+        for d in range(1, cross):
+            late_spread(d, k).start()
+        late_share(0, k).start()
+
+    def late_pass(k):
+        for d in range(1, cross):
+            late_spread(d, k).wait_recv()
+            late_share(d, k).start()
+
+    def late_lead(k, carry):
+        late_add(k)
+        return carry
+
+    lead = cols // 2
+    lax.fori_loop(0, lead, late_lead, 0)
     for d in range(1, cross):
         last_copy(d).wait_recv()
     for e in range(1, inner):
@@ -685,30 +716,28 @@
 
     def mix_early(k, carry):
         mix(0, k)
+
+        @pl.when(k >= lead)
+        def _():
+            late_add(k)
+
         return carry
 
     lax.fori_loop(0, cols, mix_early, 0)
 
-    def late_done(k):
-        for d in range(1, cross):
-            late_copy(d, k).wait()
-        value = total[mine, lane(k)]
-        for d in range(1, cross):
-            value = value + late_recv[d - 1, :, lane(k)].astype(F32)
-        acts_done[done_rows(1), lane(k)] = value.astype(BF16)
-        late_share(k).start()
-
-    def late_turn(k, carry):
-        late_done(k)
-        return carry
-
-    lax.fori_loop(0, cols, late_turn, 0)
+    for k in range(min(2, cols)):
+        late_pass(k)
     for e in range(1, inner):
         for s in (2, 3):
             gside(e, s).wait_recv()
 
     def mix_late(k, carry):
-        late_share(k).wait_recv()
+        @pl.when(k + 2 < cols)
+        def _():
+            late_pass(k + 2)
+
+        for d in range(cross):
+            late_share(d, k).wait_recv()
         mix(1, k)
         return carry
 
@@ -748,9 +777,6 @@
         value = value + held[d]
     out[...] = value[: out.shape[0], : out.shape[1]]
 
-    def left(source, sem):
-        pltpu.make_async_copy(source, source, sem).wait()
-
     left(rows_held.at[pl.ds(0, (wide - 1) * block), held_cols(0)], a2a_s.at[0])
     row_block = acts_all.at[rows(0, wi)]
 
@@ -797,18 +823,20 @@
 
     for e in range(1, inner):
         first(e).wait_send()
-        for s in range(outer):
-            gside(e, s).wait_send()
-    for d in range(1, outer):
-        second(d).wait_send()
-        gline(d).wait_send()
+        left(grads_all.at[:, 0], gy_s.at[e - 1])
+    left(second_recv, second_s.at[0])
+    left(second_recv, gz_s.at[0])
     core_copy(1).wait_send()
     for d in range(cross):
         last_copy(d).wait_send()
     for d in range(1, cross):
         done_copy(d).wait_send()
-    for k in range(cols):
-        late_share(k).wait_send()
+    f32_part, bf16_part = total.at[pl.ds(0, share)], acts_done.at[pl.ds(0, share)]
+    left(bf16_part, lshare_s.at[0])
+    for d in range(1, cross):
+        left(f32_part, late_s.at[d - 1])
+        left(bf16_part, spread_s.at[d - 1])
+        left(bf16_part, lshare_s.at[d])
     left(across.at[pl.ds(0, narrow - 1)], send_n.at[0])
     left(held.at[pl.ds(0, wide - 1)], send_w.at[0])
 
@@ -843,7 +871,6 @@
             pltpu.VMEM((tokens, columns), BF16),
             pltpu.VMEM((plane, columns), F32),
             pltpu.VMEM((cross - 1, plane // cross, columns), F32),
-            pltpu.VMEM((cross - 1, plane, columns), BF16),
             pltpu.VMEM((16, 128) if inside else (tokens, rows_out), BF16),
             pltpu.VMEM((16, 128) if inside else (rows_out, width_out), BF16),
             pltpu.VMEM((outer, block, width_out), F32),
@@ -862,35 +889,37 @@
             dma((1,)),
             dma((1,)),
             dma((wide,)),
-            dma((parts,)),
+            dma((1,)),
             dma((parts,)),
             dma((2,)),
             dma((outer,)),
             dma((outer, chunks)),
             dma((outer,)),
-            dma((outer, max(DETOUR, 1))),
+            dma((2, max(DETOUR, 1))),
             dma((inner - 1, outer,)),
             dma((inner - 1, outer, chunks,)),
             dma((inner,)),
             dma((inner,)),
+            dma((1,)),
             dma((outer,)),
+            dma((1,)),
             dma((outer,)),
-            dma((outer,)),
-            dma((outer,)),
-            dma((inner, outer,)),
-            dma((inner, outer,)),
+            dma((inner,)),
+            dma((inner - 1, outer)),
             dma((2,)),
             dma((2,)),
             dma((cross,)),
             dma((cross,)),
-            dma((cross, cols,)),
-            dma((cross, cols,)),
+            dma((cross - 1,)),
+            dma((cross - 1, cols)),
+            dma((cross - 1,)),
+            dma((cross - 1, cols)),
             dma((cross,)),
             dma((cross,)),
             dma((cross,)),
             dma((cross,)),
-            dma((cols,)),
-            dma((cols,)),
+            dma((cross,)),
+            dma((cross, cols)),
             dma((1,)),
             dma((wide,)),
             dma((1,)),

time: 92.9 us -> 92 us (level)
  no operation moved by 1% of the time
where the time goes in v4:
time: 92 us; the launch traced here: 91.9 us
  Pallas kernels  90.6 us (98%)
  local copies, waits for them, and re-layouts  1.24 us (1%)
    pallas_call x1, Pallas kernels, score(): pl.pallas_call(functools.partial(score_kernel, wide, narrow, docs), out_s...  90.6 us

profile of v4, /device:TPU:0, one launch (start us, length us, event | category | flops | bytes accessed | tf_op | source)
XLA Modules:
  0.0 91.9 jit_solution(2759727244173770151)
XLA Ops:
  0.0 90.6 %score.1 = f32[2,16]{1,0:T(2,128)} custom-call(bf16[32,7168]{1,0:T(8,128)(2,1)} %acts.1, bf16[32,8192]{1,0:T(8,128)(2,1)} %grads.1, bf16[7168,3584]{1,0:T(8,128)(2,1)} %basis_in.1, bf16[1024,2048]{1,0:T(8,128)(2,1)} %basis_out.1, bf16[2048,3584]{1,0:T(8,128)(2,1)} %eigenvalues.1, bf16[2,2048,3584]{2,1,0:T(8,128)(2,1)} %queries.1, s32[256]{0:T(256)} %ids.1), custom_call_target="tpu_custom_call" | custom-call | tf_op jit(solution)/shard_map/score/pallas_call | solution.py:861
  90.6 1.2 %copy.9 = f32[16,2]{0,1:T(2,128)} copy(f32[16,2]{0,1:T(2,128)} %bitcast.1) | data formatting | bytes 256

commit v5 on v4

--- a/solution.py
+++ b/solution.py
@@ -16,7 +16,7 @@
 PIECES = 16
 EARLY = 1
 BEFORE = 4
-AHEAD = 4
+AHEAD = 5
 DETOUR = 3
 
 

time: 92 us -> 92.1 us (level)
  no operation moved by 1% of the time
where the time goes in v5:
time: 92.1 us; the launch traced here: 91.9 us
  Pallas kernels  90.7 us (98%)
  local copies, waits for them, and re-layouts  1.24 us (1%)
    pallas_call x1, Pallas kernels, score(): pl.pallas_call(functools.partial(score_kernel, wide, narrow, docs), out_s...  90.7 us

profile of v5, /device:TPU:0, one launch (start us, length us, event | category | flops | bytes accessed | tf_op | source)
XLA Modules:
  0.0 91.9 jit_solution(380641327346813230)
XLA Ops:
  0.0 90.7 %score.1 = f32[2,16]{1,0:T(2,128)} custom-call(bf16[32,7168]{1,0:T(8,128)(2,1)} %acts.1, bf16[32,8192]{1,0:T(8,128)(2,1)} %grads.1, bf16[7168,3584]{1,0:T(8,128)(2,1)} %basis_in.1, bf16[1024,2048]{1,0:T(8,128)(2,1)} %basis_out.1, bf16[2048,3584]{1,0:T(8,128)(2,1)} %eigenvalues.1, bf16[2,2048,3584]{2,1,0:T(8,128)(2,1)} %queries.1, s32[256]{0:T(256)} %ids.1), custom_call_target="tpu_custom_call" | custom-call | tf_op jit(solution)/shard_map/score/pallas_call | solution.py:861
  90.7 1.2 %copy.9 = f32[16,2]{0,1:T(2,128)} copy(f32[16,2]{0,1:T(2,128)} %bitcast.1) | data formatting | bytes 256
